TPU v7x, 256 devices: a whole 4x4x8 slice. The times are simulated.
256 devices in a mesh: seq: 32 (over x, z), head: 8 (over y, core).
Axes of the slice: x: 4, y: 4, z: 8, core: 2. Of those that a mesh axis runs over, the one named last changes fastest.
Arguments:
- hidden_states: bfloat16 [16384, 2048], P('seq', 'head'), may hold values from -7 to 7
- proj_ba: bfloat16 [2048, 64], P('head'), may hold values from -0.125 to 0.125
- query_in: bfloat16 [16384, 2048], P('seq', 'head'), may hold values from -6 to 6
- key_in: bfloat16 [16384, 2048], P('seq', 'head'), may hold values from -6 to 6
- value_in: bfloat16 [16384, 4096], P('seq', 'head'), may hold values from -6 to 6
- conv_query: bfloat16 [4, 2048], P(None, 'head'), may hold values from -2 to 2
- conv_key: bfloat16 [4, 2048], P(None, 'head'), may hold values from -2 to 2
- convolution_value_taps: bfloat16 [4, 4096], P(None, 'head'), may hold values from -2.5 to 2.5
- decay_scale: float32 [32], P('head'), may hold values from 1 to 16
- dt_bias: float32 [32], P('head'), may hold values from -30 to -2
Outputs:
- layer_output: float32 [16384, 4096], P('seq', 'head')
All inputs are finite; a program needn't handle non-finite values.
Results may differ from a plain program's by a relative error of at most 0.0003.
Values may be sent and summed in bfloat16 or wider, within the bound.
A program may use at most 128 MiB of HBM per device.

v0:
```python
import math

import jax
import jax.numpy as jnp
from jax import lax
from jax.sharding import PartitionSpec as P

DK = 128
DV = 128
KCONV = 4
BLOCK = 128


highest = lax.Precision.HIGHEST


def passed_along(block, axis, distance):
    devices = range(lax.axis_size(axis))
    route = [(i - distance, i) for i in devices if i - distance in devices]
    return lax.ppermute(block, axis, route)


def carried_in(array, axis, combine, identity):
    count, place = (lax.axis_size(axis), lax.axis_index(axis))
    everything = jax.tree.map(lambda part: lax.all_gather(part, axis), array)
    start = jax.tree.map(
        lambda part, zero: jnp.broadcast_to(jnp.asarray(zero, part.dtype), part.shape),
        array,
        identity,
    )

    def lap(k, before):
        reached = k < place
        new = combine(before, jax.tree.map(lambda part: part[k], everything))
        return jax.tree.map(lambda a, b: jnp.where(reached, a, b), new, before)

    return lax.fori_loop(0, count, lap, start)


def causal_conv(previous, current, weights):
    padded = jnp.concatenate([previous, current], axis=0).astype(jnp.float32)
    length = current.shape[0]
    kernel = weights.astype(jnp.float32)
    summed = jnp.zeros(current.shape, jnp.float32)
    for offset in range(weights.shape[0]):
        summed = summed + kernel[offset][None, :] * lax.slice_in_dim(
            padded, offset, offset + length, axis=0
        )
    return jax.nn.silu(summed)


def unit_rows(features, head_count, factor):
    reshaped_array = features.reshape(features.shape[0], head_count, -1)
    normed = (
        reshaped_array
        * lax.rsqrt(jnp.sum(reshaped_array * reshaped_array, axis=-1, keepdims=True) + 1e-06)
        * factor
    )
    return jnp.transpose(normed, (1, 0, 2))


def block_terms(queries, key_rows, values, log_decay, write_rate):
    block_length = queries.shape[-2]
    cumulative = jnp.cumsum(log_decay, axis=-1)
    row_index = lax.broadcasted_iota(jnp.int32, (block_length, block_length), 0)
    column_index = lax.broadcasted_iota(jnp.int32, (block_length, block_length), 1)
    causal = row_index >= column_index
    strict = row_index > column_index
    spread = cumulative[..., :, None] - cumulative[..., None, :]
    decay_table = jnp.where(causal, jnp.exp(jnp.where(causal, spread, 0.0)), 0.0)
    key_dots = jnp.einsum("...td,...sd->...ts", key_rows, key_rows, precision=highest)
    lower_part = jnp.where(strict, write_rate[..., :, None] * decay_table * key_dots, 0.0)
    system = lower_part + jnp.eye(block_length, dtype=jnp.float32)
    growth = jnp.exp(cumulative)
    stacked = jnp.concatenate(
        [write_rate[..., None] * values, (write_rate * growth)[..., None] * key_rows], axis=-1
    )
    solved = jax.scipy.linalg.solve_triangular(system, stacked, lower=True, unit_diagonal=True)
    value_width = values.shape[-1]
    update_value = solved[..., :value_width]
    update_key = solved[..., value_width:]
    query_dots = jnp.einsum("...td,...sd->...ts", queries, key_rows, precision=highest)
    attend = jnp.where(causal, query_dots * decay_table, 0.0)
    scaled_query = growth[..., None] * queries
    tail_keys = jnp.exp(cumulative[..., -1:] - cumulative)[..., None] * key_rows
    end_decay = growth[..., -1]
    return (scaled_query, attend, update_value, update_key, tail_keys, end_decay)


def to_front(source):
    return jnp.moveaxis(source, 1, 0)


def apply_move(move_matrix, state_now):
    return jnp.einsum("hdf,hfe->hde", move_matrix, state_now, precision=highest)


def per_device(
    hidden_states,
    proj_ba,
    query_in,
    key_in,
    value_in,
    conv_query,
    conv_key,
    convolution_value_taps,
    decay_scale,
    dt_bias,
):
    heads_here = decay_scale.shape[0]
    local_tokens = hidden_states.shape[0]
    key_count = query_in.shape[1] // DK
    group_size = heads_here // key_count
    block_count = local_tokens // BLOCK
    query_scale = 1.0 / math.sqrt(DK)
    logits = lax.psum_scatter(
        lax.dot_general(
            proj_ba, hidden_states, (((0,), (1,)), ((), ())), preferred_element_type=jnp.float32
        ),
        "head",
        scatter_dimension=0,
        tiled=True,
    )
    log_decay = -decay_scale[:, None] * jax.nn.softplus(logits[0::2] + dt_bias[:, None])
    write_rate = jax.nn.sigmoid(logits[1::2])
    margin = KCONV - 1
    tail_rows = (
        query_in[local_tokens - margin :],
        key_in[local_tokens - margin :],
        value_in[local_tokens - margin :],
    )
    before_query, before_key, before_value = passed_along(
        (tail_rows[0], tail_rows[1], tail_rows[2]), "seq", 1
    )
    unit_query = jnp.repeat(
        unit_rows(causal_conv(before_query, query_in, conv_query), key_count, query_scale),
        group_size,
        axis=0,
    )
    unit_keys = jnp.repeat(
        unit_rows(causal_conv(before_key, key_in, conv_key), key_count, 1.0), group_size, axis=0
    )
    mixed_values = jnp.transpose(
        causal_conv(before_value, value_in, convolution_value_taps).reshape(
            local_tokens, heads_here, DV
        ),
        (1, 0, 2),
    )

    def blocks(source):
        return source.reshape(heads_here, block_count, BLOCK, source.shape[-1])

    scaled_query, attend, update_value, update_key, tail_keys, end_decay = block_terms(
        blocks(unit_query),
        blocks(unit_keys),
        blocks(mixed_values),
        log_decay.reshape(heads_here, block_count, BLOCK),
        write_rate.reshape(heads_here, block_count, BLOCK),
    )
    identity_key = jnp.eye(DK, dtype=jnp.float32)

    def local_step(carried_pair, pieces):
        state_now, transit = carried_pair
        value_part, key_part, tail_part, end_part = pieces
        errors = value_part - jnp.einsum("hcd,hde->hce", key_part, state_now, precision=highest)
        next_state = end_part[:, None, None] * state_now + jnp.einsum(
            "hcd,hce->hde", tail_part, errors, precision=highest
        )
        block_move = end_part[:, None, None] * identity_key - jnp.einsum(
            "hcd,hcf->hdf", tail_part, key_part, precision=highest
        )
        next_transit = apply_move(block_move, transit)
        return ((next_state, next_transit), (state_now, transit))

    start_pair = (
        jnp.zeros((heads_here, DK, DV), jnp.float32),
        jnp.broadcast_to(identity_key, (heads_here, DK, DK)),
    )
    (dev_state, dev_move), (start_states, start_moves) = lax.scan(
        local_step,
        start_pair,
        (to_front(update_value), to_front(update_key), to_front(tail_keys), to_front(end_decay)),
    )

    def combine(first_pair, second_pair):
        return (
            apply_move(second_pair[0], first_pair[0]),
            apply_move(second_pair[0], first_pair[1]) + second_pair[1],
        )

    neutral = (jnp.broadcast_to(identity_key, dev_move.shape), jnp.zeros_like(dev_state))
    unused, entering = carried_in((dev_move, dev_state), "seq", combine, neutral)

    def final_step(state_now, pieces):
        query_part, attend_part, value_part, key_part, tail_part, end_part = pieces
        errors = value_part - jnp.einsum("hcd,hde->hce", key_part, state_now, precision=highest)
        produced = jnp.einsum(
            "hcd,hde->hce", query_part, state_now, precision=highest
        ) + jnp.einsum("hcs,hse->hce", attend_part, errors, precision=highest)
        next_state = end_part[:, None, None] * state_now + jnp.einsum(
            "hcd,hce->hde", tail_part, errors, precision=highest
        )
        return (next_state, produced)

    unused_state, produced = lax.scan(
        final_step,
        entering,
        (
            to_front(scaled_query),
            to_front(attend),
            to_front(update_value),
            to_front(update_key),
            to_front(tail_keys),
            to_front(end_decay),
        ),
    )
    outputs = jnp.moveaxis(produced, 0, 1)
    return jnp.transpose(outputs.reshape(heads_here, local_tokens, DV), (1, 0, 2)).reshape(
        local_tokens, heads_here * DV
    )


def solution(mesh):
    placed = (
        P("seq", "head"),
        P("head", None),
        P("seq", "head"),
        P("seq", "head"),
        P("seq", "head"),
        P(None, "head"),
        P(None, "head"),
        P(None, "head"),
        P("head"),
        P("head"),
    )
    return jax.shard_map(
        per_device, mesh=mesh, in_specs=placed, out_specs=P("seq", "head"), check_vma=False
    )
```

profile of v0, /device:TPU:6, one launch (start us, length us, event | category | flops | bytes accessed | tf_op | source)
XLA Modules:
  0.0 512.4 jit_solution(14338454386088809133)
XLA Ops:
  7.3 3.8 collective-permute-start
  11.8 3.8 collective-permute-start.2
  16.3 3.8 collective-permute-start.1
  20.2 1.6 fusion.74
  30.7 1.6 copy_bitcast_fusion
  32.3 22.7 %reduce-scatter.2.cloned.1.call-done = f32[8,512]{1,0:T(8,128)} async-done(((f32[64,512]{1,0:T(8,128)}), f32[8,512]{1,0:T(8,128)}) %reduce-scatter.2.cloned.1.call-update) | async-done | bytes 16400 | tf_op jit(solution)/shard_map/reduce_scatter | solution.py:116
  58.5 3.4 fusion.53
  61.9 158.6 %custom-call.4 = f32[4,4,1,128,128]{3,4,2,1,0:T(8,128)} custom-call(f32[4,4,1,128,128]{4,3,2,1,0:T(8,128)} %fusion.53), custom_call_target="InvertDiagBlocksLowerTriangular" | custom-call | tf_op jit(solution)/shard_map/jit(_solve_triangular)/vmap(vmap())/triangular_solve | solution.py:78
  220.6 2.1 broadcast_multiply_fusion
  222.7 1.6 copy.71
  224.4 1.6 broadcast_multiply_fusion.1
  226.1 2.0 fusion.43
  229.5 10.6 %while.40 = (s32[]{:T(128)}, f32[4,128,128]{2,1,0:T(8,128)S(1)}, f32[4,128,128]{2,1,0:T(8,128)S(1)}, f32[4,4]{1,0:T(4,128)S(1)}, f32[4,4,128,128]{2,3,1,0:T(8,12...) while((s32[]{:T(128)}, f32[4,128,128]{2,1,0:T(8,128)S(1)}, ...), condition=%wide.region_4.5_spmd.clone, body=%wide.region_3.4_spmd.clone.sunk | while | flops 403144704 | bytes 4329111 | solution.py:179
  241.6 4.9 fusion.48
  246.5 89.8 %all-gather.5.cloned.1.call-done = f32[128,128,128]{2,1,0:T(8,128)} async-done(((f32[4,128,128]{2,1,0:T(8,128)}), f32[128,128,128]{2,1,0:T(8,128)}) %all-gather.5.cloned.1.call-update) | async-done | bytes 8388624 | tf_op jit(solution)/shard_map/all_gather | solution.py:25
  336.3 98.3 %all-gather.7.cloned.1.call-done = f32[128,128,128]{2,1,0:T(8,128)} async-done(((f32[4,128,128]{2,1,0:T(8,128)}), f32[128,128,128]{2,1,0:T(8,128)}) %all-gather.7.cloned.1.call-update) | async-done | bytes 8388624 | tf_op jit(solution)/shard_map/all_gather | solution.py:25
  434.6 47.5 %while.41 = (s32[]{:T(128)}, f32[4,128,128]{2,1,0:T(8,128)S(1)}, s32[]{:T(128)}, f32[32,4,128,128]{3,2,1,0:T(8,128)}, f32[32,4,128,128]{3,2,1,0:T(8,128)}, /*index=5*/s32[]{:T(128)}, s32[]{:T(128)}) while((s32[]{:T(128)}, f32[4,128,128]{2,1,0:T(8,128)S(1)}, s32[]{:T(128)}, f32[32,4,128,128]{3,2,1,0:T(8,128)}, ...), condition=%wide.region_6.7_spmd.clone, body=%wide.region_5.6_spmd.clone.sunk | while | flops 100925440 | bytes 1837671 | solution.py:37
  434.7 1.4 fusion.135
  436.2 1.4 fusion.135
  437.6 1.4 fusion.135
  439.1 1.4 fusion.135
  440.6 1.4 fusion.135
  442.1 1.4 fusion.135
  443.6 1.4 fusion.135
  445.1 1.4 fusion.135
  446.5 1.4 fusion.135
  448.0 1.4 fusion.135
  449.5 1.4 fusion.135
  451.0 1.4 fusion.135
  452.5 1.4 fusion.135
  454.0 1.4 fusion.135
  455.4 1.4 fusion.135
  456.9 1.4 fusion.135
  458.4 1.4 fusion.135
  461.4 1.4 fusion.135
  462.9 1.4 fusion.135
  464.3 1.4 fusion.135
  468.8 1.4 fusion.135
  474.7 1.4 fusion.135
  476.2 1.4 fusion.135
  479.2 1.4 fusion.135
  480.7 1.4 fusion.135
  482.1 20.9 %while.39 = (s32[]{:T(128)}, f32[4,128,128]{2,1,0:T(8,128)S(1)}, f32[4,4,128,128]{3,2,0,1:T(8,128)}, f32[4,4]{1,0:T(4,128)S(1)}, f32[4,4,128,128]{2,3,1,0:T(8,12...) while((s32[]{:T(128)}, f32[4,128,128]{2,1,0:T(8,128)S(1)}, ...), condition=%wide.region_9.10_spmd, body=%wide.region_8.9_spmd.sunk | while | flops 402915328 | bytes 3934873 | solution.py:205
  485.3 2.1 fusion.121
  490.5 2.1 fusion.121
  495.8 2.0 fusion.121
  501.0 2.1 fusion.121
  503.0 1.6 copy.85
  (160 shorter events, 52.0 us)
Async XLA Ops:
  6.5 13.6 %copy-start = (bf16[512,256]{1,0:T(8,128)(2,1)S(1)}, bf16[512,256]{1,0:T(8,128)(2,1)}, u32[]{:S(2)}) copy-start(bf16[512,256]{1,0:T(8,128)(2,1)} %param.16) | copy-start | bytes 786436
  6.5 48.5 %reduce-scatter.2.cloned.1.call-start = ((), (), s32[]{:S(2)}) async-start(), calls=%async_computation.1 | async-start | bytes 147456 | tf_op jit(solution)/shard_map/reduce_scatter | solution.py:116
  7.3 20.9 %collective-permute-start = (bf16[3,256]{1,0:T(4,128)(2,1)S(1)}, bf16[3,256]{1,0:T(4,128)(2,1)S(1)}, u32[]{:S(2)}, u32[]{:S(2)}) collective-permute-start(bf16[3,256]{1,0:T(4,128)(2,1)S(1)} %slice.109), channel_id=1, source_target_pairs={{0,8},{8,16},{16,24},{24,32},{32,40},{40,48},{48,56},{56,64},{64,7... | collective-permute-start | bytes 4616 | tf_op jit(solution)/shard_map/ppermute | solution.py:20
  11.8 13.4 %collective-permute-start.2 = (bf16[3,256]{1,0:T(4,128)(2,1)S(1)}, bf16[3,256]{1,0:T(4,128)(2,1)S(1)}, u32[]{:S(2)}, u32[]{:S(2)}) collective-permute-start(bf16[3,256]{1,0:T(4,128)(2,1)S(1)} %slice.130), channel_id=1, source_target_pairs={{0,8},{8,16},{16,24},{24,32},{32,40},{40,48},{48,56},{56,64},{64,7... | collective-permute-start | bytes 4616 | tf_op jit(solution)/shard_map/ppermute | solution.py:20
  16.3 14.0 %collective-permute-start.1 = (bf16[3,512]{1,0:T(4,128)(2,1)S(1)}, bf16[3,512]{1,0:T(4,128)(2,1)S(1)}, u32[]{:S(2)}, u32[]{:S(2)}) collective-permute-start(bf16[3,512]{1,0:T(4,128)(2,1)S(1)} %slice.119), channel_id=1, source_target_pairs={{0,8},{8,16},{16,24},{24,32},{32,40},{40,48},{48,56},{56,64},{64,7... | collective-permute-start | bytes 9224 | tf_op jit(solution)/shard_map/ppermute | solution.py:20
  21.8 314.5 %all-gather.5.cloned.1.call-start = ((), (), s32[]{:S(2)}) async-start(), calls=%async_computation.2 | async-start | bytes 8650752 | tf_op jit(solution)/shard_map/all_gather | solution.py:25
  26.5 1.7 copy-start.8
  29.5 1.0 copy-start.7
  30.7 25.1 %copy-start.9 = (f32[4]{0:T(128)S(1)}, f32[4]{0:T(128)}, u32[]{:S(2)}) copy-start(f32[4]{0:T(128)} %param.25) | copy-start | bytes 52
  58.4 162.1 %copy-start.3 = (f32[2,2,512,128]{3,2,1,0:T(8,128)}, f32[2,2,512,128]{3,2,1,0:T(8,128)S(1)}, u32[]{:S(2)}) copy-start(f32[2,2,512,128]{3,2,1,0:T(8,128)S(1)} %broadcast_in_dim.53) | copy-start | bytes 3145732
  220.6 2.2 copy-start.4
  222.7 3.3 copy-start.5
  224.4 1.7 copy-start.6
  240.1 0.7 copy-start.2
  240.1 1.0 copy-start.1
  240.9 193.8 %all-gather.7.cloned.1.call-start = ((), (), s32[]{:S(2)}) async-start(), calls=%async_computation.3 | async-start | bytes 8650752 | tf_op jit(solution)/shard_map/all_gather | solution.py:25
Sparse Core Ops, SparseCore 0:
  21.9 33.0 reduce-scatter.1
  241.0 95.2 all-gather.4
  339.2 95.3 all-gather.6
where the time goes:
time: 517 us; the launch traced here: 512 us
  waiting for transfers between devices  211 us (41%)
  other arithmetic  171 us (33%)
  matrix products  88.6 us (17%)
  local copies, waits for them, and re-layouts  15 us (3%)
  between operations  13.5 us (3%)
  starting transfers between devices  11.7 us (2%)
    all_gather x2, waiting for transfers between devices, carried_in(): everything = jax.tree.map(lambda part: lax.all_gather(part, axis), array)  188 us
    another operation x4, other arithmetic, block_terms(): jax.scipy.linalg.solve_triangular(system, stacked, lower=True, unit_diago...  159 us
    dot_general x36, matrix products, apply_move(): return jnp.einsum('hdf,hfe->hde', move_matrix, state_now, precision=highest)  47.3 us
    reduce_scatter x1, waiting for transfers between devices, per_device(): lax.psum_scatter(lax.dot_general(proj_ba, hidden_states, (((0,), (1,)), (...  22.7 us
    ppermute x3, starting transfers between devices, passed_along(): return lax.ppermute(block, axis, route)  11.4 us
  transfers between devices with their start and end apart: 6, of which 3 were waited for; matrix products, arithmetic and copies ran while one was open for 3% of the time, Pallas kernels for 0%

commit v1 on v0

v1 whole, which is shorter than its diff:
```python
import functools
import math

import jax
import jax.numpy as jnp
from jax import lax
from jax.experimental import pallas as pl
from jax.experimental.pallas import tpu as pltpu
from jax.sharding import PartitionSpec as P

DK = 128
DV = 128
KCONV = 4
C = 128
ZROW = 8
GROUP = 4
HALO = 16

MESH = pl.DeviceIdType.MESH
F32 = jnp.float32
BF16 = jnp.bfloat16


def split(a):
    hi = a.astype(BF16)
    return hi, (a - hi.astype(F32)).astype(BF16)


def mm(a, b, dims=(((1,), (0,)), ((), ()))):
    dot = functools.partial(lax.dot_general, dimension_numbers=dims, preferred_element_type=F32)
    return dot(a[0], b[0]) + (dot(a[0], b[1]) + dot(a[1], b[0]))


NT = (((1,), (1,)), ((), ()))


def iota(shape, axis):
    return lax.broadcasted_iota(jnp.int32, shape, axis)


def silu(u):
    return u / (1.0 + jnp.exp(-u))


def exchange_kernel(heads, hid, proj, q, k, v, g_out, halo_out, part, parts, tail, halo,
                    send, recv, hsend, hrecv):
    seq, head = lax.axis_index("seq"), lax.axis_index("head")
    shards = lax.axis_size("seq")
    after, before = lax.rem(seq + 1, shards), lax.rem(seq + shards - 1, shards)
    barrier = pltpu.get_barrier_semaphore()
    for o in range(1, heads):
        pl.semaphore_signal(barrier, inc=1, device_id={"head": lax.rem(head + o, heads)}, device_id_type=MESH)
    for s in (after, before):
        pl.semaphore_signal(barrier, inc=1, device_id={"seq": s}, device_id_type=MESH)

    rows = q.shape[0]
    wq, wk = q.shape[1], k.shape[1]
    tail[:, :wq] = q[rows - HALO:, :]
    tail[:, wq:wq + wk] = k[rows - HALO:, :]
    tail[:, wq + wk:] = v[rows - HALO:, :]
    logits = jnp.dot(hid[...], proj[...], preferred_element_type=F32)
    flat = jnp.transpose(logits)
    per = flat.shape[0] // heads
    for p in range(heads):
        part[p] = flat[p * per:(p + 1) * per, :]
    pl.semaphore_wait(barrier, heads + 1)

    hcopy = pltpu.make_async_remote_copy(
        src_ref=tail, dst_ref=halo, send_sem=hsend, recv_sem=hrecv,
        device_id={"seq": after}, device_id_type=MESH)
    hcopy.start()
    copies = []
    for o in range(1, heads):
        to = lax.rem(head + o, heads)
        copy = pltpu.make_async_remote_copy(
            src_ref=part.at[to], dst_ref=parts.at[o - 1], send_sem=send.at[o - 1], recv_sem=recv.at[o - 1],
            device_id={"head": to}, device_id_type=MESH)
        copy.start()
        copies.append(copy)
    total = part[head]
    for o, copy in enumerate(copies):
        copy.wait_recv()
        total = total + parts[o]
    g_out[...] = total
    hcopy.wait_recv()
    halo_out[...] = jnp.where(seq == 0, 0.0, halo[...].astype(F32)).astype(BF16)
    hcopy.wait_send()
    for copy in copies:
        copy.wait_send()


def exchange(hid, proj, q, k, v, heads):
    rows = hid.shape[0]
    per = proj.shape[1] // heads
    width = q.shape[1] + k.shape[1] + v.shape[1]
    vm = pl.BlockSpec(memory_space=pltpu.VMEM)
    return pl.pallas_call(
        functools.partial(exchange_kernel, heads),
        out_shape=(jax.ShapeDtypeStruct((per, rows), F32), jax.ShapeDtypeStruct((HALO, width), BF16)),
        in_specs=[vm] * 5,
        out_specs=(vm, vm),
        scratch_shapes=[
            pltpu.VMEM((heads, per, rows), F32),
            pltpu.VMEM((heads - 1, per, rows), F32),
            pltpu.VMEM((HALO, width), BF16),
            pltpu.VMEM((HALO, width), BF16),
            pltpu.SemaphoreType.DMA((heads - 1,)),
            pltpu.SemaphoreType.DMA((heads - 1,)),
            pltpu.SemaphoreType.DMA,
            pltpu.SemaphoreType.DMA,
        ],
        compiler_params=pltpu.CompilerParams(collective_id=0, has_side_effects=True),
        name="exchange",
    )(hid, proj, q, k, v)


def inverse(a, r, c):
    t = jnp.where(r == c, 1.0, 0.0) - jnp.where((r >> 1) == (c >> 1), a, 0.0)
    for level in range(1, 7):
        off = ((r >> (level + 1)) == (c >> (level + 1))) & ((r >> level) != (c >> level))
        ts = split(t)
        t = t - mm(ts, split(mm(split(jnp.where(off, a, 0.0)), ts)))
    return t


def local_kernel(heads, group, scale_ref, bias_ref, g, q, k, v, cq, ck, cv, halo,
                 r_out, o_out, ms_out, pad, state):
    step = pl.program_id(0)
    wq, wk = q.shape[1], k.shape[1]
    width = pad.shape[1]

    @pl.when(step == 0)
    def _():
        pad[0:8, :] = halo[HALO - 8:HALO, :].astype(F32)
        eye = jnp.where(iota((DK, DK), 0) == iota((DK, DK), 1), 1.0, 0.0)
        for h in range(heads):
            state[h, 0] = eye
            state[h, 1] = jnp.zeros((DK, DV), F32)

    @pl.when(step > 0)
    def _():
        pad[0:8, :] = pad[C:C + 8, :]

    pad[8:8 + C, :wq] = q[...].astype(F32)
    pad[8:8 + C, wq:wq + wk] = k[...].astype(F32)
    pad[8:8 + C, wq + wk:] = v[...].astype(F32)

    def conv(col, taps, tcol):
        total = None
        for j in range(KCONV):
            term = taps[j:j + 1, tcol:tcol + DK].astype(F32) * pad[5 + j:5 + j + C, col:col + DK]
            total = term if total is None else total + term
        return silu(total)

    def unit(u, factor):
        return u * (lax.rsqrt(jnp.sum(u * u, axis=-1, keepdims=True) + 1e-06) * factor)

    r, c = iota((C, C), 0), iota((C, C), 1)
    causal, strict = r >= c, r > c

    decays, rates = [], []
    for h in range(heads):
        u = g[2 * h:2 * h + 1, :] + bias_ref[h]
        e = jnp.exp(-jnp.abs(u))
        w = 1.0 + e
        log1p = jnp.where(w == 1.0, e, jnp.log(w) * (e / jnp.where(w == 1.0, 1.0, w - 1.0)))
        decays.append(-scale_ref[h] * (jnp.maximum(u, 0.0) + log1p))
        rates.append(1.0 / (1.0 + jnp.exp(-g[2 * h + 1:2 * h + 2, :])))
    ones = jnp.where(r <= c, 1.0, 0.0)
    table = jnp.concatenate(decays + rates, axis=0)
    cum = lax.dot_general(table, ones, (((1,), (0,)), ((), ())), precision=lax.Precision.HIGHEST,
                          preferred_element_type=F32)
    cum_col, rate_col = jnp.transpose(cum), jnp.transpose(table)

    for n in range(heads // group):
        queries = unit(conv(n * DK, cq, n * DK), 1.0 / math.sqrt(DK))
        keys = unit(conv(wq + n * DK, ck, n * DK), 1.0)
        keys_s = split(keys)
        queries_s = split(queries)
        kk = mm(keys_s, keys_s, NT)
        qk = mm(queries_s, keys_s, NT)
        keys_t = jnp.transpose(keys)
        for h in range(n * group, (n + 1) * group):
            values = conv(wq + wk + h * DV, cv, h * DV)
            gc, gr = cum_col[:, h:h + 1], cum[h:h + 1, :]
            beta = rate_col[:, heads + h:heads + h + 1]
            decay = jnp.where(causal, jnp.exp(jnp.where(causal, gc - gr, 0.0)), 0.0)
            solve = inverse(jnp.where(strict, beta * decay * kk, 0.0), r, c)
            growth = jnp.exp(gc)
            solve_s = split(solve)
            wu = mm(solve_s, split(jnp.concatenate([(beta * growth) * keys, beta * values], axis=1)))
            x = jnp.concatenate([state[h, 0], state[h, 1]], axis=1)
            x_s = split(x)
            y = mm(split(-wu[:, :DK]), x_s)
            y = jnp.concatenate([y[:, :DK], y[:, DK:] + wu[:, DK:]], axis=1)
            y_s = split(y)
            out = mm(split(growth * queries), x_s) + mm(split(decay * qk), y_s)
            r_out[:, h * DK:(h + 1) * DK] = out[:, :DK]
            o_out[:, h * DV:(h + 1) * DV] = out[:, DK:]
            last = cum[h:h + 1, C - 1:C]
            x = jnp.exp(last) * x + mm(split(keys_t * jnp.exp(last - gr)), y_s)
            state[h, 0] = x[:, :DK]
            state[h, 1] = x[:, DK:]

    ms_out[...] = state[...]


def local(scale, bias, g, q, k, v, cq, ck, cv, halo):
    heads = scale.shape[0]
    rows = q.shape[0]
    group = heads // (q.shape[1] // DK)
    smem = pl.BlockSpec(memory_space=pltpu.SMEM)

    def rowblock(a):
        return pl.BlockSpec((C, a.shape[1]), lambda i: (i, 0))

    def whole(a):
        return pl.BlockSpec(a.shape, lambda i: (0,) * a.ndim)

    width = q.shape[1] + k.shape[1] + v.shape[1]
    return pl.pallas_call(
        functools.partial(local_kernel, heads, group),
        grid=(rows // C,),
        out_shape=(
            jax.ShapeDtypeStruct((rows, heads * DK), F32),
            jax.ShapeDtypeStruct((rows, heads * DV), F32),
            jax.ShapeDtypeStruct((heads, 2, DK, DV), F32),
        ),
        in_specs=[smem, smem, pl.BlockSpec((g.shape[0], C), lambda i: (0, i)), rowblock(q), rowblock(k),
                  rowblock(v), whole(cq), whole(ck), whole(cv), whole(halo)],
        out_specs=(
            pl.BlockSpec((C, heads * DK), lambda i: (i, 0)),
            pl.BlockSpec((C, heads * DV), lambda i: (i, 0)),
            pl.BlockSpec((heads, 2, DK, DV), lambda i: (0, 0, 0, 0)),
        ),
        scratch_shapes=[pltpu.VMEM((C + 8, width), F32), pltpu.VMEM((heads, 2, DK, DV), F32)],
        compiler_params=pltpu.CompilerParams(dimension_semantics=("arbitrary",)),
        name="local",
    )(scale, bias, g, q, k, v, cq, ck, cv, halo)


def wide(ref, *at):
    return jnp.concatenate([ref[(*at, 0)], ref[(*at, 1)]], axis=1)


def then(later_move, later_state, x):
    y = mm(split(later_move), split(x))
    return y[:, :DK], y[:, DK:] + later_state


def scan_kernel(rows_x, ms, e_out, gathered, prefix, mine, other, total, rows, entry, staged, arrived,
                send1, recv1, send2, recv2, send3, recv3, send4, recv4):
    seq = lax.axis_index("seq")
    z = lax.rem(seq, ZROW)
    x = seq // ZROW
    half = z // GROUP
    place = lax.rem(z, GROUP)
    own = jnp.where(half == 0, place, GROUP - 1 - place)
    base = seq - place
    mirror = x * ZROW + (ZROW - 1 - z)

    def owned(p):
        return jnp.where(half == 0, p, GROUP - 1 - p)

    barrier = pltpu.get_barrier_semaphore()
    for o in range(1, GROUP):
        pl.semaphore_signal(barrier, inc=1, device_id={"seq": base + lax.rem(place + o, GROUP)}, device_id_type=MESH)
    pl.semaphore_signal(barrier, inc=1, device_id={"seq": mirror}, device_id_type=MESH)
    for o in range(1, rows_x):
        pl.semaphore_signal(barrier, inc=1, device_id={"seq": lax.rem(x + o, rows_x) * ZROW + z}, device_id_type=MESH)
    pl.semaphore_wait(barrier, GROUP - 1 + 1 + rows_x - 1)

    first = []
    for o in range(1, GROUP):
        p = lax.rem(place + o, GROUP)
        copy = pltpu.make_async_remote_copy(
            src_ref=ms.at[owned(p)], dst_ref=gathered.at[place], send_sem=send1.at[o - 1],
            recv_sem=recv1.at[place], device_id={"seq": base + p}, device_id_type=MESH)
        copy.start()
        first.append(copy)
    gathered[place] = ms[own]
    def arrive(t):
        @pl.when(place != t)
        def _():
            pltpu.make_async_remote_copy(
                src_ref=ms.at[0], dst_ref=gathered.at[t], send_sem=send1.at[0], recv_sem=recv1.at[t],
                device_id={"seq": mirror}, device_id_type=MESH).wait_recv()

    arrive(0)
    prefix[1] = gathered[0]
    for t in range(1, GROUP):
        arrive(t)
        move, state = then(gathered[t, 0], gathered[t, 1], wide(prefix, t))
        if t < GROUP - 1:
            prefix[t + 1, 0], prefix[t + 1, 1] = move, state
        else:
            mine[0], mine[1] = move, state

    second = pltpu.make_async_remote_copy(
        src_ref=mine, dst_ref=other, send_sem=send2, recv_sem=recv2,
        device_id={"seq": mirror}, device_id_type=MESH)
    second.start()
    second.wait_recv()
    early = half == 0
    a_move, a_state = jnp.where(early, mine[0], other[0]), jnp.where(early, mine[1], other[1])
    b_move, b_state = jnp.where(early, other[0], mine[0]), jnp.where(early, other[1], mine[1])
    total[0], total[1] = then(b_move, b_state, jnp.concatenate([a_move, a_state], axis=1))

    def to_row(d):
        return pltpu.make_async_remote_copy(
            src_ref=total, dst_ref=rows.at[x], send_sem=send3.at[d], recv_sem=recv3.at[x],
            device_id={"seq": d * ZROW + z}, device_id_type=MESH)

    for d in range(1, rows_x):
        @pl.when(x < d)
        def _(d=d):
            to_row(d).start()
    entry[...] = jnp.zeros_like(entry)
    for t in range(rows_x - 1):
        @pl.when(t < x)
        def _(t=t):
            pltpu.make_async_remote_copy(
                src_ref=total, dst_ref=rows.at[t], send_sem=send3.at[0], recv_sem=recv3.at[t],
                device_id={"seq": mirror}, device_id_type=MESH).wait_recv()
            if t == 0:
                entry[...] = rows[0, 1]
            else:
                entry[...] = mm(split(rows[t, 0]), split(entry[...])) + rows[t, 1]
    for d in range(1, rows_x):
        @pl.when(x < d)
        def _(d=d):
            to_row(d).wait_send()

    e = entry[...]
    e = jnp.where(early, e, mm(split(a_move), split(e)) + a_state)
    e_s = split(e)
    staged[0] = e
    for t in range(1, GROUP):
        staged[t] = mm(split(prefix[t, 0]), e_s) + prefix[t, 1]
    last = []
    for o in range(1, GROUP):
        p = lax.rem(place + o, GROUP)
        copy = pltpu.make_async_remote_copy(
            src_ref=staged.at[p], dst_ref=arrived.at[own], send_sem=send4.at[o - 1], recv_sem=recv4.at[own],
            device_id={"seq": base + p}, device_id_type=MESH)
        copy.start()
        last.append(copy)
    arrived[own] = staged[place]
    for h in range(GROUP):
        @pl.when(own != h)
        def _(h=h):
            pltpu.make_async_remote_copy(
                src_ref=staged.at[0], dst_ref=arrived.at[h], send_sem=send4.at[0], recv_sem=recv4.at[h],
                device_id={"seq": mirror}, device_id_type=MESH).wait_recv()
    e_out[...] = arrived[...]
    for copy in first + [second] + last:
        copy.wait_send()


def entering(ms, shards):
    heads = ms.shape[0]
    rows_x = shards // ZROW
    assert heads == GROUP
    vm = pl.BlockSpec(memory_space=pltpu.VMEM)
    dma = pltpu.SemaphoreType.DMA
    pair = (2, DK, DV)
    return pl.pallas_call(
        functools.partial(scan_kernel, rows_x),
        out_shape=jax.ShapeDtypeStruct((heads, DK, DV), F32),
        in_specs=[vm],
        out_specs=vm,
        scratch_shapes=[
            pltpu.VMEM((GROUP, *pair), F32),
            pltpu.VMEM((GROUP, *pair), F32),
            pltpu.VMEM(pair, F32),
            pltpu.VMEM(pair, F32),
            pltpu.VMEM(pair, F32),
            pltpu.VMEM((rows_x, *pair), F32),
            pltpu.VMEM((DK, DV), F32),
            pltpu.VMEM((GROUP, DK, DV), F32),
            pltpu.VMEM((GROUP, DK, DV), F32),
            dma((GROUP - 1,)), dma((GROUP,)),
            dma, dma,
            dma((rows_x,)), dma((rows_x,)),
            dma((GROUP - 1,)), dma((GROUP,)),
        ],
        compiler_params=pltpu.CompilerParams(collective_id=1, has_side_effects=True),
        name="entering",
    )(ms)


def final_kernel(heads, r, o, e, out):
    for h in range(heads):
        cols = slice(h * DK, (h + 1) * DK)
        out[:, cols] = o[:, cols] + mm(split(r[:, cols]), split(e[h]))


def final(r, o, e):
    rows, width = r.shape
    spec = pl.BlockSpec((C, width), lambda i: (i, 0))
    return pl.pallas_call(
        functools.partial(final_kernel, e.shape[0]),
        grid=(rows // C,),
        out_shape=jax.ShapeDtypeStruct(o.shape, F32),
        in_specs=[spec, spec, pl.BlockSpec(e.shape, lambda i: (0, 0, 0))],
        out_specs=spec,
        compiler_params=pltpu.CompilerParams(dimension_semantics=("arbitrary",)),
        name="final",
    )(r, o, e)


def solution(mesh):
    heads, shards = mesh.shape["head"], mesh.shape["seq"]

    def per_device(hid, proj, q, k, v, cq, ck, cv, scale, bias):
        g, halo = exchange(hid, proj, q, k, v, heads)
        r, o, ms = local(scale, bias, g, q, k, v, cq, ck, cv, halo)
        return final(r, o, entering(ms, shards))

    placed = (
        P("seq", "head"), P("head", None), P("seq", "head"), P("seq", "head"), P("seq", "head"),
        P(None, "head"), P(None, "head"), P(None, "head"), P("head"), P("head"),
    )
    return jax.shard_map(per_device, mesh=mesh, in_specs=placed, out_specs=P("seq", "head"), check_vma=False)
```

time: 517 us -> 104 us (0.20)
  waiting for transfers between devices: 211 us -> 0 us
  other arithmetic: 171 us -> 0 us
  Pallas kernels: 0 us -> 102 us
  matrix products: 88.6 us -> 0 us
  local copies, waits for them, and re-layouts: 15 us -> 1.49 us
  between operations: 13.5 us -> 0.02 us
  starting transfers between devices: 11.7 us -> 0 us
    all_gather x2 -> x0, waiting for transfers between devices: 188 us -> none  [carried_in(): everything = jax.tree.map(lambda part: lax.all_gather(part, axis), array)]
    another operation x5 -> x0, other arithmetic: 160 us -> none  [the longest x4 159 us: block_terms(): jax.scipy.linalg.solve_triangular(system, stacked, lower=True, unit_diago...]
    pallas_call x0 -> x4, Pallas kernels: none -> 102 us  [the longest x1 47.4 us: local(): pl.pallas_call(functools.partial(local_kernel, heads, group), grid=(rows...]
    dot_general x67 -> x0, matrix products: 86.5 us -> none  [the longest x36 47.3 us: apply_move(): return jnp.einsum('hdf,hfe->hde', move_matrix, state_now, precision=highest)]
    reduce_scatter x1 -> x0, waiting for transfers between devices: 22.7 us -> none  [per_device(): lax.psum_scatter(lax.dot_general(proj_ba, hidden_states, (((0,), (1,)), (...]
    ppermute x3 -> x0, starting transfers between devices: 11.4 us -> none  [passed_along(): return lax.ppermute(block, axis, route)]
    slice x10 -> x0, local copies, waits for them, and re-layouts: 6.42 us -> none  [the longest x3 2.51 us: causal_conv(): kernel[offset][None, :]]
  transfers between devices with their start and end apart: 6 -> 0, of which waited for: 3 -> 0; matrix products, arithmetic and copies ran while one was open for 3% -> 0% of each run, Pallas kernels for 0% -> 0%
where the time goes in v1:
time: 104 us
  Pallas kernels  102 us (98%)
  local copies, waits for them, and re-layouts  1.49 us (1%)
    pallas_call x1, Pallas kernels, local(): pl.pallas_call(functools.partial(local_kernel, heads, group), grid=(rows...  47.4 us
    pallas_call x1, Pallas kernels, entering(): pl.pallas_call(functools.partial(scan_kernel, rows_x), out_shape=jax.Shap...  37.3 us
    pallas_call x1, Pallas kernels, exchange(): pl.pallas_call(functools.partial(exchange_kernel, heads), out_shape=(jax....  13.5 us
    pallas_call x1, Pallas kernels, final(): pl.pallas_call(functools.partial(final_kernel, e.shape[0]), grid=(rows //...  4.12 us

profile of v1, /device:TPU:6, one launch (start us, length us, event | category | flops | bytes accessed | tf_op | source)
XLA Modules:
  0.0 103.8 jit_solution(16973066890478880765)
XLA Ops:
  0.0 1.5 %copy.11.proj = bf16[256,64]{1,0:T(8,128)(2,1)} copy(bf16[256,64]{0,1:T(8,128)(2,1)} %param.11) | data formatting | bytes 65536 | tf_op args[1]
  1.5 13.5 %exchange.1 = (f32[8,512]{1,0:T(8,128)}, bf16[16,1024]{1,0:T(8,128)(2,1)}) custom-call(bf16[512,256]{1,0:T(8,128)(2,1)} %hid.1, bf16[256,64]{1,0:T(8,128)(2,1)} %copy.11.proj, bf16[512,256]{1,0:T(8,128)(2,1)} %q.3, bf16[512,256]{1,0:T(8,128)(2,1)} %k.3, bf16[512,512]{1,0:T(8,128)(2,1)} %v.3), custom_call_target="tpu_custom_call" | custom-call | tf_op jit(solution)/shard_map/exchange/pallas_call | solution.py:97
  15.0 47.4 %local.1 = (f32[512,512]{1,0:T(8,128)}, f32[512,512]{1,0:T(8,128)}, f32[4,2,128,128]{3,2,1,0:T(8,128)}) custom-call(f32[4]{0:T(128)} %scale_ref.1, f32[4]{0:T(128)} %bias_ref.1, f32[8,512]{1,0:T(8,128)} %get-tuple-element.10.g, bf16[512,256]{1,0:T(8,128)(2,1)} %q.3, bf16[512,256]{1,0:T(8,128)(2,1)} %k.3, bf16[512,512]{1,0:T(8,128)(2,1)} %v.3, ...), custom_call_target="tpu_custom_call" | custom-call | tf_op jit(solution)/shard_map/local/pallas_call | solution.py:221
  62.3 37.3 %entering.1.e = f32[4,128,128]{2,1,0:T(8,128)} custom-call(f32[4,2,128,128]{3,2,1,0:T(8,128)} %get-tuple-element.14.ms), custom_call_target="tpu_custom_call" | custom-call | tf_op jit(solution)/shard_map/entering/pallas_call | solution.py:367
  99.7 4.1 %final.1 = f32[512,512]{1,0:T(8,128)} custom-call(f32[512,512]{1,0:T(8,128)} %get-tuple-element.12.r, f32[512,512]{1,0:T(8,128)} %get-tuple-element.13.o, f32[4,128,128]{2,1,0:T(8,128)} %entering.1.e), custom_call_target="tpu_custom_call" | custom-call | tf_op jit(solution)/shard_map/final/pallas_call | solution.py:401

commit v2 on v1

--- a/solution.py
+++ b/solution.py
@@ -114,13 +114,25 @@
     )(hid, proj, q, k, v)
 
 
-def inverse(a, r, c):
-    t = jnp.where(r == c, 1.0, 0.0) - jnp.where((r >> 1) == (c >> 1), a, 0.0)
-    for level in range(1, 7):
+def inverses(systems, r, c):
+    lane, sub = iota((8, C), 1), iota((8, C), 0)
+    group = lane >> 3
+    solved = []
+    for a in systems:
+        packed = a[0:8, :]
+        for j in range(1, C // 8):
+            packed = jnp.where(group == j, a[8 * j:8 * j + 8, :], packed)
+        t = jnp.where((lane & 7) == sub, 1.0, 0.0)
+        for m in range(7):
+            factor = jnp.take_along_axis(packed, (lane & ~7) + m, axis=1)
+            t = t - factor * t[m:m + 1, :]
+        solved.append(jnp.concatenate([jnp.where(group == j, t, 0.0) for j in range(C // 8)], axis=0))
+    for level in range(3, 7):
         off = ((r >> (level + 1)) == (c >> (level + 1))) & ((r >> level) != (c >> level))
-        ts = split(t)
-        t = t - mm(ts, split(mm(split(jnp.where(off, a, 0.0)), ts)))
-    return t
+        parts = [split(t) for t in solved]
+        inner = [mm(split(jnp.where(off, a, 0.0)), ts) for a, ts in zip(systems, parts)]
+        solved = [t - mm(ts, split(p)) for t, ts, p in zip(solved, parts, inner)]
+    return solved
 
 
 def local_kernel(heads, group, scale_ref, bias_ref, g, q, k, v, cq, ck, cv, halo,
@@ -172,35 +184,39 @@
                           preferred_element_type=F32)
     cum_col, rate_col = jnp.transpose(cum), jnp.transpose(table)
 
-    for n in range(heads // group):
-        queries = unit(conv(n * DK, cq, n * DK), 1.0 / math.sqrt(DK))
-        keys = unit(conv(wq + n * DK, ck, n * DK), 1.0)
-        keys_s = split(keys)
-        queries_s = split(queries)
-        kk = mm(keys_s, keys_s, NT)
-        qk = mm(queries_s, keys_s, NT)
-        keys_t = jnp.transpose(keys)
-        for h in range(n * group, (n + 1) * group):
-            values = conv(wq + wk + h * DV, cv, h * DV)
-            gc, gr = cum_col[:, h:h + 1], cum[h:h + 1, :]
-            beta = rate_col[:, heads + h:heads + h + 1]
-            decay = jnp.where(causal, jnp.exp(jnp.where(causal, gc - gr, 0.0)), 0.0)
-            solve = inverse(jnp.where(strict, beta * decay * kk, 0.0), r, c)
-            growth = jnp.exp(gc)
-            solve_s = split(solve)
-            wu = mm(solve_s, split(jnp.concatenate([(beta * growth) * keys, beta * values], axis=1)))
-            x = jnp.concatenate([state[h, 0], state[h, 1]], axis=1)
-            x_s = split(x)
-            y = mm(split(-wu[:, :DK]), x_s)
-            y = jnp.concatenate([y[:, :DK], y[:, DK:] + wu[:, DK:]], axis=1)
-            y_s = split(y)
-            out = mm(split(growth * queries), x_s) + mm(split(decay * qk), y_s)
-            r_out[:, h * DK:(h + 1) * DK] = out[:, :DK]
-            o_out[:, h * DV:(h + 1) * DV] = out[:, DK:]
-            last = cum[h:h + 1, C - 1:C]
-            x = jnp.exp(last) * x + mm(split(keys_t * jnp.exp(last - gr)), y_s)
-            state[h, 0] = x[:, :DK]
-            state[h, 1] = x[:, DK:]
+    key_heads = range(heads // group)
+    queries = [unit(conv(n * DK, cq, n * DK), 1.0 / math.sqrt(DK)) for n in key_heads]
+    keys = [unit(conv(wq + n * DK, ck, n * DK), 1.0) for n in key_heads]
+    keys_s = [split(x) for x in keys]
+    kk = [mm(x, x, NT) for x in keys_s]
+    qk = [mm(split(queries[n]), keys_s[n], NT) for n in key_heads]
+    keys_t = [jnp.transpose(x) for x in keys]
+    every = range(heads)
+    betas = [rate_col[:, heads + h:heads + h + 1] for h in every]
+    decay = []
+    for h in every:
+        gap = cum_col[:, h:h + 1] - cum[h:h + 1, :]
+        decay.append(jnp.where(causal, jnp.exp(jnp.where(causal, gap, 0.0)), 0.0))
+    solved = inverses([jnp.where(strict, betas[h] * decay[h] * kk[h // group], 0.0) for h in every], r, c)
+    growth = [jnp.exp(cum_col[:, h:h + 1]) for h in every]
+    right = []
+    for h in every:
+        values = conv(wq + wk + h * DV, cv, h * DV)
+        right.append(split(jnp.concatenate([(betas[h] * growth[h]) * keys[h // group], betas[h] * values], axis=1)))
+    wu = [mm(split(solved[h]), right[h]) for h in every]
+    xs = [jnp.concatenate([state[h, 0], state[h, 1]], axis=1) for h in every]
+    xs_s = [split(x) for x in xs]
+    ys = [mm(split(-wu[h][:, :DK]), xs_s[h]) for h in every]
+    ys_s = [split(jnp.concatenate([ys[h][:, :DK], ys[h][:, DK:] + wu[h][:, DK:]], axis=1)) for h in every]
+    for h in every:
+        last = cum[h:h + 1, C - 1:C]
+        x = jnp.exp(last) * xs[h] + mm(split(keys_t[h // group] * jnp.exp(last - cum[h:h + 1, :])), ys_s[h])
+        state[h, 0] = x[:, :DK]
+        state[h, 1] = x[:, DK:]
+    for h in every:
+        out = mm(split(growth[h] * queries[h // group]), xs_s[h]) + mm(split(decay[h] * qk[h // group]), ys_s[h])
+        r_out[:, h * DK:(h + 1) * DK] = out[:, :DK]
+        o_out[:, h * DV:(h + 1) * DV] = out[:, DK:]
 
     ms_out[...] = state[...]
 

time: 104 us -> 73.3 us (0.70)
  Pallas kernels: 102 us -> 71.5 us
    pallas_call x1, Pallas kernels: 47.4 us -> 16.5 us  [local(): pl.pallas_call(functools.partial(local_kernel, heads, group), grid=(rows...]
where the time goes in v2:
time: 73.3 us; the launch traced here: 73 us
  Pallas kernels  71.5 us (98%)
  local copies, waits for them, and re-layouts  1.49 us (2%)
    pallas_call x1, Pallas kernels, entering(): pl.pallas_call(functools.partial(scan_kernel, rows_x), out_shape=jax.Shap...  37.3 us
    pallas_call x1, Pallas kernels, local(): pl.pallas_call(functools.partial(local_kernel, heads, group), grid=(rows...  16.5 us
    pallas_call x1, Pallas kernels, exchange(): pl.pallas_call(functools.partial(exchange_kernel, heads), out_shape=(jax....  13.5 us
    pallas_call x1, Pallas kernels, final(): pl.pallas_call(functools.partial(final_kernel, e.shape[0]), grid=(rows //...  4.12 us
    unnamed x1, local copies, waits for them, and re-layouts  1.49 us

profile of v2, /device:TPU:6, one launch (start us, length us, event | category | flops | bytes accessed | tf_op | source)
XLA Modules:
  0.0 73.0 jit_solution(9154226129010746648)
XLA Ops:
  0.0 1.5 %copy.11.proj = bf16[256,64]{1,0:T(8,128)(2,1)} copy(bf16[256,64]{0,1:T(8,128)(2,1)} %param.11) | data formatting | bytes 65536 | tf_op args[1]
  1.5 13.5 %exchange.1 = (f32[8,512]{1,0:T(8,128)}, bf16[16,1024]{1,0:T(8,128)(2,1)}) custom-call(bf16[512,256]{1,0:T(8,128)(2,1)} %hid.1, bf16[256,64]{1,0:T(8,128)(2,1)} %copy.11.proj, bf16[512,256]{1,0:T(8,128)(2,1)} %q.3, bf16[512,256]{1,0:T(8,128)(2,1)} %k.3, bf16[512,512]{1,0:T(8,128)(2,1)} %v.3), custom_call_target="tpu_custom_call" | custom-call | tf_op jit(solution)/shard_map/exchange/pallas_call | solution.py:97
  15.0 16.5 %local.1 = (f32[512,512]{1,0:T(8,128)}, f32[512,512]{1,0:T(8,128)}, f32[4,2,128,128]{3,2,1,0:T(8,128)}) custom-call(f32[4]{0:T(128)} %scale_ref.1, f32[4]{0:T(128)} %bias_ref.1, f32[8,512]{1,0:T(8,128)} %get-tuple-element.10.g, bf16[512,256]{1,0:T(8,128)(2,1)} %q.3, bf16[512,256]{1,0:T(8,128)(2,1)} %k.3, bf16[512,512]{1,0:T(8,128)(2,1)} %v.3, ...), custom_call_target="tpu_custom_call" | custom-call | tf_op jit(solution)/shard_map/local/pallas_call | solution.py:237
  31.5 37.3 %entering.1.e = f32[4,128,128]{2,1,0:T(8,128)} custom-call(f32[4,2,128,128]{3,2,1,0:T(8,128)} %get-tuple-element.14.ms), custom_call_target="tpu_custom_call" | custom-call | tf_op jit(solution)/shard_map/entering/pallas_call | solution.py:383
  68.9 4.1 %final.1 = f32[512,512]{1,0:T(8,128)} custom-call(f32[512,512]{1,0:T(8,128)} %get-tuple-element.12.r, f32[512,512]{1,0:T(8,128)} %get-tuple-element.13.o, f32[4,128,128]{2,1,0:T(8,128)} %entering.1.e), custom_call_target="tpu_custom_call" | custom-call | tf_op jit(solution)/shard_map/final/pallas_call | solution.py:417

commit v3 on v0

v3 whole, which is shorter than its diff:
```python
import functools
import math

import jax
import jax.numpy as jnp
from jax import lax
from jax.experimental import pallas as pl
from jax.experimental.pallas import tpu as pltpu
from jax.sharding import PartitionSpec as P

DK = 128
DV = 128
KCONV = 4
C = 128
ZROW = 8
GROUP = 4
HALO = 16

MESH = pl.DeviceIdType.MESH
F32 = jnp.float32
BF16 = jnp.bfloat16


def split(a):
    hi = a.astype(BF16)
    return hi, (a - hi.astype(F32)).astype(BF16)


NN = (((1,), (0,)), ((), ()))
NT = (((1,), (1,)), ((), ()))


def mm(a, b, dims=NN):
    dot = functools.partial(lax.dot_general, dimension_numbers=dims, preferred_element_type=F32)
    if dims is NN and a[0].shape[1] == 128:
        pair = jnp.concatenate(a, axis=1)
        hi, lo = (jnp.concatenate([x, x], axis=0) for x in b)
        return dot(pair, hi) + dot(pair, lo)
    return dot(a[0], b[0]) + (dot(a[0], b[1]) + dot(a[1], b[0]))


def iota(shape, axis):
    return lax.broadcasted_iota(jnp.int32, shape, axis)


def silu(u):
    return u / (1.0 + jnp.exp(-u))


def inverses(systems, r, c):
    lane, sub = iota((8, C), 1), iota((8, C), 0)
    group = lane >> 3
    solved = []
    for a in systems:
        packed = a[0:8, :]
        for j in range(1, C // 8):
            packed = jnp.where(group == j, a[8 * j:8 * j + 8, :], packed)
        t = jnp.where((lane & 7) == sub, 1.0, 0.0)
        for m in range(7):
            factor = jnp.take_along_axis(packed, (lane & ~7) + m, axis=1)
            t = t - factor * t[m:m + 1, :]
        solved.append(jnp.concatenate([jnp.where(group == j, t, 0.0) for j in range(C // 8)], axis=0))
    for level in range(3, 7):
        off = ((r >> (level + 1)) == (c >> (level + 1))) & ((r >> level) != (c >> level))
        parts = [split(t) for t in solved]
        inner = [mm(split(jnp.where(off, a, 0.0)), ts) for a, ts in zip(systems, parts)]
        solved = [t - mm(ts, split(p)) for t, ts, p in zip(solved, parts, inner)]
    return solved


def wide(ref, *at):
    return jnp.concatenate([ref[(*at, 0)], ref[(*at, 1)]], axis=1)


def then(later_move, later_state, x):
    y = mm(split(later_move), split(x))
    return y[:, :DK], y[:, DK:] + later_state


SEAT = (0, 3, 1, 2)


def owned_at(p):
    return jnp.where(p == 0, 0, jnp.where(p == GROUP - 1, 1, p + 1))


def whole_kernel(peers, heads, rows_x, scale, bias, hid, proj, q, k, v, cq, ck, cv, out,
                 part, parts, halo, pad, uq, uk, uv, kk, qk, attend, wu, xs, ms, rhi, rlo,
                 gathered, prefix, mine, other, total, tin, ein, entry, enext, full, staged, arrived,
                 send, recv, hsend, hrecv, send1, recv1, send2, recv2, send3, recv3, send4, recv4):
    seq, head = lax.axis_index("seq"), lax.axis_index("head")
    shards = rows_x * ZROW
    z, x = lax.rem(seq, ZROW), seq // ZROW
    half, place = z // GROUP, lax.rem(z, GROUP)
    first_half = half == 0
    base = seq - place
    mirror = x * ZROW + (ZROW - 1 - z)
    after, before = lax.rem(seq + 1, shards), lax.rem(seq + shards - 1, shards)
    own = owned_at(jnp.where(first_half, place, GROUP - 1 - place))
    seats = [jnp.where(first_half, SEAT[h], GROUP - 1 - SEAT[h]) for h in range(heads)]
    rows, wq, wk = q.shape[0], q.shape[1], k.shape[1]
    blocks, key_heads = rows // C, wq // DK
    group = heads // key_heads
    shared = functools.partial(pltpu.make_async_remote_copy, device_id_type=MESH)

    barrier = pltpu.get_barrier_semaphore()
    for o in range(1, peers):
        pl.semaphore_signal(barrier, inc=1, device_id={"head": lax.rem(head + o, peers)}, device_id_type=MESH)
    others = [after, before, mirror]
    others += [base + lax.rem(place + o, GROUP) for o in range(1, GROUP)]
    others += [lax.rem(x + o, rows_x) * ZROW + z for o in range(1, rows_x)]
    for s in others:
        pl.semaphore_signal(barrier, inc=1, device_id={"seq": s}, device_id_type=MESH)

    flat = lax.dot_general(proj[...], hid[...], NT, preferred_element_type=F32)
    per = flat.shape[0] // peers
    for p in range(peers):
        part[p] = flat[p * per:(p + 1) * per, :]
    pl.semaphore_wait(barrier, peers - 1 + len(others))
    copies = []
    for o in range(1, peers):
        to = lax.rem(head + o, peers)
        copies.append(shared(src_ref=part.at[to], dst_ref=parts.at[o - 1], send_sem=send.at[o - 1],
                             recv_sem=recv.at[o - 1], device_id={"head": to}))
    columns = [(q, 0), (k, wq), (v, wq + wk)]
    halos = []
    for i, (src, col) in enumerate(columns):
        halos.append(shared(src_ref=src.at[pl.ds(rows - HALO, HALO)],
                            dst_ref=halo.at[:, pl.ds(col, src.shape[1])],
                            send_sem=hsend.at[i], recv_sem=hrecv.at[i], device_id={"seq": after}))
    for copy in halos + copies:
        copy.start()

    for src, col in columns:
        pad[8:8 + rows, col:col + src.shape[1]] = src[...].astype(F32)

    def conv(b, col, taps, tcol):
        summed = None
        for j in range(KCONV):
            term = taps[j:j + 1, tcol:tcol + DK].astype(F32) * pad[5 + j + b * C:5 + j + (b + 1) * C, col:col + DK]
            summed = term if summed is None else summed + term
        return silu(summed)

    def unit(u, factor):
        return u * (lax.rsqrt(jnp.sum(u * u, axis=-1, keepdims=True) + 1e-06) * factor)

    def features(b):
        at = slice(b * C, (b + 1) * C)
        for n in range(key_heads):
            cols = slice(n * DK, (n + 1) * DK)
            queries = unit(conv(b, n * DK, cq, n * DK), 1.0 / math.sqrt(DK))
            keys = unit(conv(b, wq + n * DK, ck, n * DK), 1.0)
            uq[at, cols], uk[at, cols] = queries, keys
            keys_s = split(keys)
            kk[n, b] = mm(keys_s, keys_s, NT)
            qk[n, b] = mm(split(queries), keys_s, NT)
        for h in range(heads):
            uv[at, h * DV:(h + 1) * DV] = conv(b, wq + wk + h * DV, cv, h * DV)

    for b in range(1, blocks):
        features(b)
    for copy in halos:
        copy.wait_recv()
    pad[0:8, :] = jnp.where(seq == 0, 0.0, halo[HALO - 8:HALO, :].astype(F32))
    features(0)

    g = part[head]
    for o, copy in enumerate(copies):
        copy.wait_recv()
        g = g + parts[o]

    r, c = iota((C, C), 0), iota((C, C), 1)
    causal, strict = r >= c, r > c
    decays, rates = [], []
    for h in range(heads):
        u = g[2 * h:2 * h + 1, :] + bias[h]
        e = jnp.exp(-jnp.abs(u))
        w = 1.0 + e
        log1p = jnp.where(w == 1.0, e, jnp.log(w) * (e / jnp.where(w == 1.0, 1.0, w - 1.0)))
        decays.append(-scale[h] * (jnp.maximum(u, 0.0) + log1p))
        rates.append(1.0 / (1.0 + jnp.exp(-g[2 * h + 1:2 * h + 2, :])))
    table = jnp.concatenate(decays + rates, axis=0)
    width = table.shape[0]
    table = jnp.concatenate([table[:, b * C:(b + 1) * C] for b in range(blocks)], axis=0)
    cum = lax.dot_general(table, jnp.where(r <= c, 1.0, 0.0), NN, precision=lax.Precision.HIGHEST,
                          preferred_element_type=F32)
    cum_col, rate_col = jnp.transpose(cum), jnp.transpose(table)

    def decay_row(h, b):
        return cum[b * width + h:b * width + h + 1, :]

    def decay_col(h, b):
        return cum_col[:, b * width + h:b * width + h + 1]

    def maps(n):
        every = [(h, b) for b in range(blocks) for h in range(n * group, (n + 1) * group)]
        cols = slice(n * DK, (n + 1) * DK)
        keys = [uk[b * C:(b + 1) * C, cols] for b in range(blocks)]
        systems, betas = [], []
        for h, b in every:
            gap = decay_col(h, b) - decay_row(h, b)
            decay = jnp.where(causal, jnp.exp(jnp.where(causal, gap, 0.0)), 0.0)
            i = b * width + heads + h
            beta = rate_col[:, i:i + 1]
            attend[h, b] = decay * qk[n, b]
            systems.append(jnp.where(strict, beta * decay * kk[n, b], 0.0))
            betas.append(beta)
        solved = inverses(systems, r, c)
        right = []
        for (h, b), beta in zip(every, betas):
            values = uv[b * C:(b + 1) * C, h * DV:(h + 1) * DV]
            right.append(split(jnp.concatenate(
                [(beta * jnp.exp(decay_col(h, b))) * keys[b], beta * values], axis=1)))
        solutions = [mm(split(t), y) for t, y in zip(solved, right)]
        keys_t = [jnp.transpose(y) for y in keys]
        eye = jnp.where(r == c, 1.0, 0.0)
        steps = {}
        for (h, b), y in zip(every, solutions):
            wu[h, b] = y
            last = cum[b * width + h:b * width + h + 1, C - 1:C]
            pair = mm(split(keys_t[b] * jnp.exp(last - decay_row(h, b))), split(y))
            steps[h, b] = (jnp.exp(last) * eye - pair[:, :DK], pair[:, DK:])
        for h in range(n * group, (n + 1) * group):
            now = jnp.concatenate(steps[h, 0], axis=1)
            for b in range(1, blocks):
                xs[h, b - 1] = now
                move, state = then(*steps[h, b], now)
                now = jnp.concatenate([move, state], axis=1)
            ms[h, 0], ms[h, 1] = now[:, :DK], now[:, DK:]

    def to_owner(h):
        return shared(src_ref=ms.at[h], dst_ref=gathered.at[place], send_sem=send1.at[h],
                      recv_sem=recv1.at[place], device_id={"seq": base + seats[h]})

    def hand_over(n):
        for h in range(n * group, (n + 1) * group):
            @pl.when(place != seats[h])
            def _(h=h):
                to_owner(h).start()

            @pl.when(place == seats[h])
            def _(h=h):
                gathered[place] = ms[h]

    def responses(n):
        for h in range(n * group, (n + 1) * group):
            cols = slice(h * DK, (h + 1) * DK)
            for b in range(blocks):
                at = slice(b * C, (b + 1) * C)
                y = wu[h, b]
                queries = jnp.exp(decay_col(h, b)) * uq[at, n * DK:(n + 1) * DK]
                if b == 0:
                    got = mm(split(attend[h, b]), split(y))
                    response, rest = queries - got[:, :DK], got[:, DK:]
                else:
                    now = xs[h, b - 1]
                    z = mm(split(y[:, :DK]), split(now))
                    y = jnp.concatenate([-z[:, :DK], y[:, DK:] - z[:, DK:]], axis=1)
                    got = mm(split(jnp.concatenate([queries, attend[h, b]], axis=1)),
                             split(jnp.concatenate([now, y], axis=0)))
                    response, rest = got[:, :DK], got[:, DK:]
                rhi[at, cols], rlo[at, cols] = split(response)
                out[at, cols] = rest

    maps(0)
    hand_over(0)
    maps(1)
    hand_over(1)
    responses(0)

    def arrive(t):
        @pl.when(place != t)
        def _():
            shared(src_ref=ms.at[0], dst_ref=gathered.at[t], send_sem=send1.at[0], recv_sem=recv1.at[t],
                   device_id={"seq": mirror}).wait_recv()

    arrive(0)
    prefix[0, 0], prefix[0, 1] = gathered[0, 0], gathered[0, 1]
    for t in range(1, GROUP):
        arrive(t)
        move, state = then(gathered[t, 0], gathered[t, 1], wide(prefix, t - 1))
        if t < GROUP - 1:
            prefix[t, 0], prefix[t, 1] = move, state
        else:
            mine[0], mine[1] = move, state

    second = shared(src_ref=mine, dst_ref=other, send_sem=send2, recv_sem=recv2, device_id={"seq": mirror})
    second.start()
    responses(1)
    second.wait_recv()
    a_move, a_state = jnp.where(first_half, mine[0], other[0]), jnp.where(first_half, mine[1], other[1])
    b_move, b_state = jnp.where(first_half, other[0], mine[0]), jnp.where(first_half, other[1], mine[1])
    total[0], total[1] = then(b_move, b_state, jnp.concatenate([a_move, a_state], axis=1))

    def to_row(src, dst, to, i, arrived_at):
        return shared(src_ref=src, dst_ref=dst, send_sem=send3.at[i], recv_sem=recv3.at[arrived_at],
                      device_id={"seq": to * ZROW + z})

    @pl.when(x == 0)
    def _():
        to_row(total.at[1], ein, 1, 0, 0).start()

    @pl.when(x == 2)
    def _():
        to_row(total, tin, 3, 0, 1).start()

    eye = jnp.where(r == c, 1.0, 0.0)
    begin = jnp.concatenate([jnp.where(first_half, eye, a_move), jnp.where(first_half, 0.0, a_state)], axis=1)
    full[0] = begin
    for t in range(1, GROUP):
        full[t] = jnp.concatenate(then(prefix[t - 1, 0], prefix[t - 1, 1], begin), axis=1)

    @pl.when(x == 0)
    def _():
        entry[...] = jnp.zeros_like(entry)

    @pl.when(x > 0)
    def _():
        to_row(total.at[1], ein, 1, 0, 0).wait_recv()

    @pl.when(x == 1)
    def _():
        enext[...] = mm(split(total[0]), split(ein[...])) + total[1]
        to_row(enext, ein, 3, 0, 0).start()
        to_row(enext, ein, 2, 1, 0).start()

    @pl.when((x == 1) | (x == 2))
    def _():
        entry[...] = ein[...]

    @pl.when(x == 3)
    def _():
        to_row(total, tin, 3, 0, 1).wait_recv()
        entry[...] = mm(split(tin[0]), split(ein[...])) + tin[1]

    e_s = split(entry[...])
    for t in range(GROUP):
        staged[t] = mm(split(full[t, :, :DK]), e_s) + full[t, :, DK:]
    last = []
    for o in range(1, GROUP):
        p = lax.rem(place + o, GROUP)
        last.append(shared(src_ref=staged.at[p], dst_ref=arrived.at[own], send_sem=send4.at[o - 1],
                           recv_sem=recv4.at[own], device_id={"seq": base + p}))
    for copy in last:
        copy.start()
    arrived[own] = staged[place]
    for h in range(heads):
        @pl.when(own != h)
        def _(h=h):
            shared(src_ref=staged.at[0], dst_ref=arrived.at[h], send_sem=send4.at[0], recv_sem=recv4.at[h],
                   device_id={"seq": mirror}).wait_recv()
        cols = slice(h * DK, (h + 1) * DK)
        out[:, cols] = out[:, cols] + mm((rhi[:, cols], rlo[:, cols]), split(arrived[h]))

    for copy in copies + halos + [second] + last:
        copy.wait_send()
    for h in range(heads):
        @pl.when(place != seats[h])
        def _(h=h):
            to_owner(h).wait_send()

    @pl.when(x == 0)
    def _():
        to_row(total.at[1], ein, 1, 0, 0).wait_send()

    @pl.when(x == 1)
    def _():
        to_row(enext, ein, 3, 0, 0).wait_send()
        to_row(enext, ein, 2, 1, 0).wait_send()

    @pl.when(x == 2)
    def _():
        to_row(total, tin, 3, 0, 1).wait_send()


def solution(mesh):
    peers, shards = mesh.shape["head"], mesh.shape["seq"]
    rows_x = shards // ZROW
    assert rows_x == 4 and shards == rows_x * ZROW

    def per_device(hid, proj, q, k, v, cq, ck, cv, scale, bias):
        heads, rows = scale.shape[0], q.shape[0]
        key_heads, blocks = q.shape[1] // DK, rows // C
        assert heads == GROUP and rows == blocks * C
        width = q.shape[1] + k.shape[1] + v.shape[1]
        per = proj.shape[1] // peers
        vm, smem = pl.BlockSpec(memory_space=pltpu.VMEM), pl.BlockSpec(memory_space=pltpu.SMEM)
        dma, pair, square = pltpu.SemaphoreType.DMA, (2, DK, DV), (C, C)

        def f32(*shape):
            return pltpu.VMEM(shape, F32)

        return pl.pallas_call(
            functools.partial(whole_kernel, peers, heads, rows_x),
            out_shape=jax.ShapeDtypeStruct((rows, heads * DV), F32),
            in_specs=[smem] * 2 + [vm] * 8,
            out_specs=vm,
            scratch_shapes=[
                f32(peers, per, rows), f32(peers - 1, per, rows), pltpu.VMEM((HALO, width), BF16),
                f32(rows + 8, width), f32(*q.shape), f32(*k.shape), f32(*v.shape),
                f32(key_heads, blocks, *square), f32(key_heads, blocks, *square),
                f32(heads, blocks, *square), f32(heads, blocks, C, DK + DV),
                f32(heads, blocks - 1, DK, DK + DV), f32(heads, *pair),
                pltpu.VMEM((rows, heads * DK), BF16), pltpu.VMEM((rows, heads * DK), BF16),
                f32(GROUP, *pair), f32(GROUP - 1, *pair), f32(*pair), f32(*pair), f32(*pair), f32(*pair),
                f32(DK, DV), f32(DK, DV), f32(DK, DV), f32(GROUP, DK, DK + DV),
                f32(GROUP, DK, DV), f32(GROUP, DK, DV),
                dma((peers - 1,)), dma((peers - 1,)), dma((3,)), dma((3,)),
                dma((heads,)), dma((GROUP,)), dma, dma, dma((2,)), dma((2,)),
                dma((GROUP - 1,)), dma((GROUP,)),
            ],
            compiler_params=pltpu.CompilerParams(collective_id=0, has_side_effects=True),
            name="delta",
        )(scale, bias, hid, jnp.transpose(proj), q, k, v, cq, ck, cv)

    placed = (
        P("seq", "head"), P("head", None), P("seq", "head"), P("seq", "head"), P("seq", "head"),
        P(None, "head"), P(None, "head"), P(None, "head"), P("head"), P("head"),
    )
    return jax.shard_map(per_device, mesh=mesh, in_specs=placed, out_specs=P("seq", "head"), check_vma=False)
```

time: 517 us -> 54.2 us (0.10)
  waiting for transfers between devices: 211 us -> 0 us
  other arithmetic: 171 us -> 0 us
  matrix products: 88.6 us -> 0 us
  Pallas kernels: 0 us -> 51.8 us
  between operations: 13.5 us -> 0.01 us
  local copies, waits for them, and re-layouts: 15 us -> 2.26 us
  starting transfers between devices: 11.7 us -> 0 us
    all_gather x2 -> x0, waiting for transfers between devices: 188 us -> none  [carried_in(): everything = jax.tree.map(lambda part: lax.all_gather(part, axis), array)]
    another operation x5 -> x0, other arithmetic: 160 us -> none  [the longest x4 159 us: block_terms(): jax.scipy.linalg.solve_triangular(system, stacked, lower=True, unit_diago...]
    dot_general x67 -> x0, matrix products: 86.5 us -> none  [the longest x36 47.3 us: apply_move(): return jnp.einsum('hdf,hfe->hde', move_matrix, state_now, precision=highest)]
    pallas_call x0 -> x1, Pallas kernels: none -> 51.8 us  [per_device(): pl.pallas_call(functools.partial(whole_kernel, peers, heads, rows_x), out...]
    reduce_scatter x1 -> x0, waiting for transfers between devices: 22.7 us -> none  [per_device(): lax.psum_scatter(lax.dot_general(proj_ba, hidden_states, (((0,), (1,)), (...]
    ppermute x3 -> x0, starting transfers between devices: 11.4 us -> none  [passed_along(): return lax.ppermute(block, axis, route)]
    slice x10 -> x0, local copies, waits for them, and re-layouts: 6.42 us -> none  [the longest x3 2.51 us: causal_conv(): kernel[offset][None, :]]
  transfers between devices with their start and end apart: 6 -> 0, of which waited for: 3 -> 0; matrix products, arithmetic and copies ran while one was open for 3% -> 0% of each run, Pallas kernels for 0% -> 0%
where the time goes in v3:
time: 54.2 us; the launch traced here: 54 us
  Pallas kernels  51.8 us (96%)
  local copies, waits for them, and re-layouts  2.26 us (4%)
    pallas_call x1, Pallas kernels, per_device(): pl.pallas_call(functools.partial(whole_kernel, peers, heads, rows_x), out...  51.8 us
    unnamed x1, local copies, waits for them, and re-layouts  2.26 us

profile of v3, /device:TPU:6, one launch (start us, length us, event | category | flops | bytes accessed | tf_op | source)
XLA Modules:
  0.0 54.0 jit_solution(12251450738649322484)
XLA Ops:
  0.0 51.8 %delta.1 = f32[512,512]{1,0:T(8,128)} custom-call(f32[4]{0:T(128)} %scale.1, f32[4]{0:T(128)} %bias.1, bf16[512,256]{1,0:T(8,128)(2,1)} %hid.1, bf16[64,256]{1,0:T(8,128)(2,1)} %bitcast.1, bf16[512,256]{1,0:T(8,128)(2,1)} %q.1, bf16[512,256]{1,0:T(8,128)(2,1)} %k.1, bf16[512,512]{1,0:T(8,128)(2,1)} %v.1, bf16[4,256]{1,0:T(4,128)(2,1)} %cq.1, ...), custom_call_target="tpu_custom_call" | custom-call | tf_op jit(solution)/shard_map/delta/pallas_call | solution.py:393
  51.8 2.3 %copy.12 = f32[512,512]{1,0:T(8,128)} copy(f32[512,512]{1,0:T(8,128)} %delta.1) | data formatting | bytes 2097152

commit v4 on v3

--- a/solution.py
+++ b/solution.py
@@ -84,9 +84,10 @@
     return jnp.where(p == 0, 0, jnp.where(p == GROUP - 1, 1, p + 1))
 
 
-def whole_kernel(peers, heads, rows_x, scale, bias, hid, proj, q, k, v, cq, ck, cv, out,
+def whole_kernel(peers, heads, rows_x, scale, bias, cq, ck, cv, hid_in, proj_in, q_in, k_in, v_in, out,
+                 hid, proj, q, k, v, load,
                  part, parts, halo, pad, uq, uk, uv, kk, qk, attend, wu, xs, ms, rhi, rlo,
-                 gathered, prefix, mine, other, total, tin, ein, entry, enext, full, staged, arrived,
+                 gathered, prefix, mine, other, total, tin, ein, begin, enext, full, staged, arrived,
                  send, recv, hsend, hrecv, send1, recv1, send2, recv2, send3, recv3, send4, recv4):
     seq, head = lax.axis_index("seq"), lax.axis_index("head")
     shards = rows_x * ZROW
@@ -112,10 +113,18 @@
     for s in others:
         pl.semaphore_signal(barrier, inc=1, device_id={"seq": s}, device_id_type=MESH)
 
+    loads = [pltpu.make_async_copy(src, dst, load.at[i]) for i, (src, dst) in enumerate(
+        [(hid_in, hid), (proj_in, proj), (q_in, q), (k_in, k), (v_in, v)])]
+    for copy in loads:
+        copy.start()
+    for copy in loads[:2]:
+        copy.wait()
     flat = lax.dot_general(proj[...], hid[...], NT, preferred_element_type=F32)
     per = flat.shape[0] // peers
     for p in range(peers):
         part[p] = flat[p * per:(p + 1) * per, :]
+    for copy in loads[2:]:
+        copy.wait()
     pl.semaphore_wait(barrier, peers - 1 + len(others))
     copies = []
     for o in range(1, peers):
@@ -275,22 +284,37 @@
                    device_id={"seq": mirror}).wait_recv()
 
     arrive(0)
+    arrive(1)
+    early = jnp.concatenate(then(gathered[1, 0], gathered[1, 1], wide(gathered, 0)), axis=1)
+    arrive(2)
+    arrive(3)
+    late = then(gathered[3, 0], gathered[3, 1], wide(gathered, 2))
+    mine[0], mine[1] = then(*late, early)
+
+    def to_mirror(i):
+        return shared(src_ref=mine.at[i], dst_ref=other.at[i], send_sem=send2.at[i], recv_sem=recv2.at[i],
+                      device_id={"seq": mirror})
+
+    lead = jnp.where(first_half, 1, 0)
+    to_mirror(lead).start()
+    to_mirror(1 - lead).start()
     prefix[0, 0], prefix[0, 1] = gathered[0, 0], gathered[0, 1]
-    for t in range(1, GROUP):
-        arrive(t)
-        move, state = then(gathered[t, 0], gathered[t, 1], wide(prefix, t - 1))
-        if t < GROUP - 1:
-            prefix[t, 0], prefix[t, 1] = move, state
-        else:
-            mine[0], mine[1] = move, state
-
-    second = shared(src_ref=mine, dst_ref=other, send_sem=send2, recv_sem=recv2, device_id={"seq": mirror})
-    second.start()
+    prefix[1, 0], prefix[1, 1] = early[:, :DK], early[:, DK:]
+    prefix[2, 0], prefix[2, 1] = then(gathered[2, 0], gathered[2, 1], early)
     responses(1)
-    second.wait_recv()
-    a_move, a_state = jnp.where(first_half, mine[0], other[0]), jnp.where(first_half, mine[1], other[1])
-    b_move, b_state = jnp.where(first_half, other[0], mine[0]), jnp.where(first_half, other[1], mine[1])
-    total[0], total[1] = then(b_move, b_state, jnp.concatenate([a_move, a_state], axis=1))
+
+    @pl.when(first_half)
+    def _():
+        to_mirror(0).wait_recv()
+        y = mm(split(other[0]), split(wide(mine)))
+        total[0] = y[:, :DK]
+        to_mirror(1).wait_recv()
+        total[1] = y[:, DK:] + other[1]
+
+    @pl.when(half == 1)
+    def _():
+        to_mirror(1).wait_recv()
+        total[1] = mm(split(mine[0]), split(other[1])) + mine[1]
 
     def to_row(src, dst, to, i, arrived_at):
         return shared(src_ref=src, dst_ref=dst, send_sem=send3.at[i], recv_sem=recv3.at[arrived_at],
@@ -300,19 +324,33 @@
     def _():
         to_row(total.at[1], ein, 1, 0, 0).start()
 
+    @pl.when(half == 1)
+    def _():
+        to_mirror(0).wait_recv()
+        total[0] = mm(split(mine[0]), split(other[0]))
+
     @pl.when(x == 2)
     def _():
         to_row(total, tin, 3, 0, 1).start()
 
     eye = jnp.where(r == c, 1.0, 0.0)
-    begin = jnp.concatenate([jnp.where(first_half, eye, a_move), jnp.where(first_half, 0.0, a_state)], axis=1)
-    full[0] = begin
+    begin[0] = jnp.where(first_half, eye, other[0])
+    begin[1] = jnp.where(first_half, 0.0, other[1])
+
+    @pl.when(x == 3)
+    def _():
+        to_row(total, tin, 3, 0, 1).wait_recv()
+        begin[0], begin[1] = then(begin[0], begin[1], wide(tin))
+
+    start_s = split(wide(begin))
+    full[0] = wide(begin)
     for t in range(1, GROUP):
-        full[t] = jnp.concatenate(then(prefix[t - 1, 0], prefix[t - 1, 1], begin), axis=1)
+        y = mm(split(prefix[t - 1, 0]), start_s)
+        full[t] = jnp.concatenate([y[:, :DK], y[:, DK:] + prefix[t - 1, 1]], axis=1)
 
     @pl.when(x == 0)
     def _():
-        entry[...] = jnp.zeros_like(entry)
+        ein[...] = jnp.zeros_like(ein)
 
     @pl.when(x > 0)
     def _():
@@ -324,25 +362,19 @@
         to_row(enext, ein, 3, 0, 0).start()
         to_row(enext, ein, 2, 1, 0).start()
 
-    @pl.when((x == 1) | (x == 2))
-    def _():
-        entry[...] = ein[...]
-
-    @pl.when(x == 3)
-    def _():
-        to_row(total, tin, 3, 0, 1).wait_recv()
-        entry[...] = mm(split(tin[0]), split(ein[...])) + tin[1]
-
-    e_s = split(entry[...])
-    for t in range(GROUP):
+    e_s = split(ein[...])
+
+    def stage(t):
         staged[t] = mm(split(full[t, :, :DK]), e_s) + full[t, :, DK:]
+
     last = []
     for o in range(1, GROUP):
         p = lax.rem(place + o, GROUP)
+        stage(p)
         last.append(shared(src_ref=staged.at[p], dst_ref=arrived.at[own], send_sem=send4.at[o - 1],
                            recv_sem=recv4.at[own], device_id={"seq": base + p}))
-    for copy in last:
-        copy.start()
+        last[-1].start()
+    stage(place)
     arrived[own] = staged[place]
     for h in range(heads):
         @pl.when(own != h)
@@ -352,7 +384,7 @@
         cols = slice(h * DK, (h + 1) * DK)
         out[:, cols] = out[:, cols] + mm((rhi[:, cols], rlo[:, cols]), split(arrived[h]))
 
-    for copy in copies + halos + [second] + last:
+    for copy in copies + halos + [to_mirror(0), to_mirror(1)] + last:
         copy.wait_send()
     for h in range(heads):
         @pl.when(place != seats[h])
@@ -384,6 +416,7 @@
         assert heads == GROUP and rows == blocks * C
         width = q.shape[1] + k.shape[1] + v.shape[1]
         per = proj.shape[1] // peers
+        proj = jnp.transpose(proj)
         vm, smem = pl.BlockSpec(memory_space=pltpu.VMEM), pl.BlockSpec(memory_space=pltpu.SMEM)
         dma, pair, square = pltpu.SemaphoreType.DMA, (2, DK, DV), (C, C)
 
@@ -393,9 +426,10 @@
         return pl.pallas_call(
             functools.partial(whole_kernel, peers, heads, rows_x),
             out_shape=jax.ShapeDtypeStruct((rows, heads * DV), F32),
-            in_specs=[smem] * 2 + [vm] * 8,
+            in_specs=[smem] * 2 + [vm] * 3 + [pl.BlockSpec(memory_space=pltpu.HBM)] * 5,
             out_specs=vm,
             scratch_shapes=[
+                *(pltpu.VMEM(a.shape, BF16) for a in (hid, proj, q, k, v)), dma((5,)),
                 f32(peers, per, rows), f32(peers - 1, per, rows), pltpu.VMEM((HALO, width), BF16),
                 f32(rows + 8, width), f32(*q.shape), f32(*k.shape), f32(*v.shape),
                 f32(key_heads, blocks, *square), f32(key_heads, blocks, *square),
@@ -403,15 +437,15 @@
                 f32(heads, blocks - 1, DK, DK + DV), f32(heads, *pair),
                 pltpu.VMEM((rows, heads * DK), BF16), pltpu.VMEM((rows, heads * DK), BF16),
                 f32(GROUP, *pair), f32(GROUP - 1, *pair), f32(*pair), f32(*pair), f32(*pair), f32(*pair),
-                f32(DK, DV), f32(DK, DV), f32(DK, DV), f32(GROUP, DK, DK + DV),
+                f32(DK, DV), f32(*pair), f32(DK, DV), f32(GROUP, DK, DK + DV),
                 f32(GROUP, DK, DV), f32(GROUP, DK, DV),
                 dma((peers - 1,)), dma((peers - 1,)), dma((3,)), dma((3,)),
-                dma((heads,)), dma((GROUP,)), dma, dma, dma((2,)), dma((2,)),
+                dma((heads,)), dma((GROUP,)), dma((2,)), dma((2,)), dma((2,)), dma((2,)),
                 dma((GROUP - 1,)), dma((GROUP,)),
             ],
             compiler_params=pltpu.CompilerParams(collective_id=0, has_side_effects=True),
             name="delta",
-        )(scale, bias, hid, jnp.transpose(proj), q, k, v, cq, ck, cv)
+        )(scale, bias, cq, ck, cv, hid, proj, q, k, v)
 
     placed = (
         P("seq", "head"), P("head", None), P("seq", "head"), P("seq", "head"), P("seq", "head"),

time: 54.2 us -> 53.5 us (0.987)
  Pallas kernels: 51.8 us -> 51 us
    pallas_call x1, Pallas kernels: 51.8 us -> 51 us  [per_device(): pl.pallas_call(functools.partial(whole_kernel, peers, heads, rows_x), out...]
where the time goes in v4:
time: 53.5 us; the launch traced here: 53.3 us
  Pallas kernels  51 us (95%)
  local copies, waits for them, and re-layouts  2.26 us (4%)
    pallas_call x1, Pallas kernels, per_device(): pl.pallas_call(functools.partial(whole_kernel, peers, heads, rows_x), out...  51 us
    unnamed x1, local copies, waits for them, and re-layouts  2.26 us

profile of v4, /device:TPU:6, one launch (start us, length us, event | category | flops | bytes accessed | tf_op | source)
XLA Modules:
  0.0 53.3 jit_solution(16788088753203235308)
XLA Ops:
  0.0 51.0 %delta.1 = f32[512,512]{1,0:T(8,128)} custom-call(f32[4]{0:T(128)} %scale.1, f32[4]{0:T(128)} %bias.1, bf16[4,256]{1,0:T(4,128)(2,1)} %cq.1, bf16[4,256]{1,0:T(4,128)(2,1)} %ck.1, bf16[4,512]{1,0:T(4,128)(2,1)} %cv.1, bf16[512,256]{1,0:T(8,128)(2,1)} %hid_in.1, bf16[64,256]{1,0:T(8,128)(2,1)} %bitcast.1, bf16[512,256]{1,0:T(8,128)(2,1)} %q_in.1, ...), custom_call_target="tpu_custom_call" | custom-call | tf_op jit(solution)/shard_map/delta/pallas_call | solution.py:426
  51.0 2.3 %copy.12 = f32[512,512]{1,0:T(8,128)} copy(f32[512,512]{1,0:T(8,128)} %delta.1) | data formatting | bytes 2097152

commit v5 on v4

--- a/solution.py
+++ b/solution.py
@@ -14,6 +14,7 @@
 C = 128
 ZROW = 8
 GROUP = 4
+BASE = 8
 HALO = 16
 
 MESH = pl.DeviceIdType.MESH
@@ -47,24 +48,44 @@
     return u / (1.0 + jnp.exp(-u))
 
 
-def inverses(systems, r, c):
-    lane, sub = iota((8, C), 1), iota((8, C), 0)
-    group = lane >> 3
+def inverses(systems):
+    lane, sub = iota((BASE, C), 1), iota((BASE, C), 0)
+    group, within = lane // BASE, lane & (BASE - 1)
     solved = []
     for a in systems:
-        packed = a[0:8, :]
-        for j in range(1, C // 8):
-            packed = jnp.where(group == j, a[8 * j:8 * j + 8, :], packed)
-        t = jnp.where((lane & 7) == sub, 1.0, 0.0)
-        for m in range(7):
-            factor = jnp.take_along_axis(packed, (lane & ~7) + m, axis=1)
-            t = t - factor * t[m:m + 1, :]
-        solved.append(jnp.concatenate([jnp.where(group == j, t, 0.0) for j in range(C // 8)], axis=0))
-    for level in range(3, 7):
-        off = ((r >> (level + 1)) == (c >> (level + 1))) & ((r >> level) != (c >> level))
+        packed = a[0:BASE, :]
+        for j in range(1, C // BASE):
+            packed = jnp.where(group == j, a[BASE * j:BASE * (j + 1), :], packed)
+        tops = [jnp.where(within[i:i + 8] == sub[i:i + 8], 1.0, 0.0) for i in range(0, BASE, 8)]
+        for m in range(BASE - 1):
+            row = tops[m // 8][m % 8:m % 8 + 1, :]
+            for i in range((m + 1) // 8, BASE // 8):
+                factor = jnp.take_along_axis(packed[8 * i:8 * i + 8], (lane[:8] - within[:8]) + m, axis=1)
+                tops[i] = tops[i] - factor * row
+        t = jnp.concatenate(tops, axis=0)
+        solved.append(jnp.concatenate([jnp.where(group == j, t, 0.0) for j in range(C // BASE)], axis=0))
+    size = BASE
+    while size < C:
+        count = C // (2 * size)
+
+        def lower(x):
+            return jnp.concatenate([x[(2 * j + 1) * size:(2 * j + 2) * size] for j in range(count)], axis=0)
+
+        def weave(upper, low):
+            pieces = []
+            for j in range(count):
+                pieces.append(upper[2 * j * size:(2 * j + 1) * size])
+                pieces.append(low[j * size:(j + 1) * size])
+            return jnp.concatenate(pieces, axis=0)
+
+        rows, cols = iota((C // 2, C), 0) // size, iota((C // 2, C), 1) // size
+        left = cols == 2 * rows
         parts = [split(t) for t in solved]
-        inner = [mm(split(jnp.where(off, a, 0.0)), ts) for a, ts in zip(systems, parts)]
-        solved = [t - mm(ts, split(p)) for t, ts, p in zip(solved, parts, inner)]
+        inner = [mm(split(jnp.where(left, lower(a), 0.0)), ts) for a, ts in zip(systems, parts)]
+        zeros = jnp.zeros((C, C), F32)
+        step = [mm(split(lower(t)), split(weave(zeros, p))) for t, p in zip(solved, inner)]
+        solved = [weave(t, lower(t) - y) for t, y in zip(solved, step)]
+        size *= 2
     return solved
 
 
@@ -214,7 +235,7 @@
             attend[h, b] = decay * qk[n, b]
             systems.append(jnp.where(strict, beta * decay * kk[n, b], 0.0))
             betas.append(beta)
-        solved = inverses(systems, r, c)
+        solved = inverses(systems)
         right = []
         for (h, b), beta in zip(every, betas):
             values = uv[b * C:(b + 1) * C, h * DV:(h + 1) * DV]
@@ -443,9 +464,9 @@
                 dma((heads,)), dma((GROUP,)), dma((2,)), dma((2,)), dma((2,)), dma((2,)),
                 dma((GROUP - 1,)), dma((GROUP,)),
             ],
-            compiler_params=pltpu.CompilerParams(collective_id=0, has_side_effects=True),
+            compiler_params=pltpu.CompilerParams(collective_id=0, has_side_effects=True, vmem_limit_bytes=40 * 1024 * 1024),
             name="delta",
-        )(scale, bias, cq, ck, cv, hid, proj, q, k, v)
+        )(*(pltpu.with_memory_space_constraint(a, pltpu.HBM) for a in (scale, bias, cq, ck, cv, hid, proj, q, k, v)))
 
     placed = (
         P("seq", "head"), P("head", None), P("seq", "head"), P("seq", "head"), P("seq", "head"),

time: 53.5 us -> 50.1 us (0.936)
  Pallas kernels: 51 us -> 48.9 us
  local copies, waits for them, and re-layouts: 2.26 us -> 0.97 us
    pallas_call x1, Pallas kernels: 51 us -> 48.9 us  [per_device(): pl.pallas_call(functools.partial(whole_kernel, peers, heads, rows_x), out...]
    unnamed x1, local copies, waits for them, and re-layouts: 2.26 us -> 0.97 us
where the time goes in v5:
time: 50.1 us; the launch traced here: 49.9 us
  Pallas kernels  48.9 us (98%)
  local copies, waits for them, and re-layouts  0.97 us (2%)
    pallas_call x1, Pallas kernels, per_device(): pl.pallas_call(functools.partial(whole_kernel, peers, heads, rows_x), out...  48.9 us

profile of v5, /device:TPU:6, one launch (start us, length us, event | category | flops | bytes accessed | tf_op | source)
XLA Modules:
  0.0 49.9 jit_solution(1932558949652424389)
XLA Ops:
  0.0 48.9 %delta.1 = f32[512,512]{1,0:T(8,128)S(1)} custom-call(f32[4]{0:T(128)} %scale.1, f32[4]{0:T(128)} %bias.1, bf16[4,256]{1,0:T(4,128)(2,1)} %cq.1, bf16[4,256]{1,0:T(4,128)(2,1)} %ck.1, bf16[4,512]{1,0:T(4,128)(2,1)} %cv.1, bf16[512,256]{1,0:T(8,128)(2,1)} %hid_in.1, bf16[64,256]{1,0:T(8,128)(2,1)} %bitcast.1, bf16[512,256]{1,0:T(8,128)(2,1)} %q_in.1, ...), custom_call_target="tpu_custom_call" | custom-call | tf_op jit(solution)/shard_map/delta/pallas_call | solution.py:447
  49.0 1.0 %copy.12 = f32[512,512]{1,0:T(8,128)} copy(f32[512,512]{1,0:T(8,128)S(1)} %delta.1) | data formatting | bytes 2097152

commit v6 on v5

--- a/solution.py
+++ b/solution.py
@@ -105,32 +105,20 @@
     return jnp.where(p == 0, 0, jnp.where(p == GROUP - 1, 1, p + 1))
 
 
-def whole_kernel(peers, heads, rows_x, scale, bias, cq, ck, cv, hid_in, proj_in, q_in, k_in, v_in, out,
-                 hid, proj, q, k, v, load,
-                 part, parts, halo, pad, uq, uk, uv, kk, qk, attend, wu, xs, ms, rhi, rlo,
-                 gathered, prefix, mine, other, total, tin, ein, begin, enext, full, staged, arrived,
-                 send, recv, hsend, hrecv, send1, recv1, send2, recv2, send3, recv3, send4, recv4):
+def features_kernel(peers, heads, cq, ck, cv, hid_in, proj_in, q_in, k_in, v_in,
+                    g_out, uq, uk, uv, kk, qk,
+                    hid, proj, q, k, v, load, part, parts, halo, pad, send, recv, hsend, hrecv):
     seq, head = lax.axis_index("seq"), lax.axis_index("head")
-    shards = rows_x * ZROW
-    z, x = lax.rem(seq, ZROW), seq // ZROW
-    half, place = z // GROUP, lax.rem(z, GROUP)
-    first_half = half == 0
-    base = seq - place
-    mirror = x * ZROW + (ZROW - 1 - z)
+    shards = lax.axis_size("seq")
     after, before = lax.rem(seq + 1, shards), lax.rem(seq + shards - 1, shards)
-    own = owned_at(jnp.where(first_half, place, GROUP - 1 - place))
-    seats = [jnp.where(first_half, SEAT[h], GROUP - 1 - SEAT[h]) for h in range(heads)]
     rows, wq, wk = q.shape[0], q.shape[1], k.shape[1]
     blocks, key_heads = rows // C, wq // DK
-    group = heads // key_heads
     shared = functools.partial(pltpu.make_async_remote_copy, device_id_type=MESH)
 
     barrier = pltpu.get_barrier_semaphore()
     for o in range(1, peers):
         pl.semaphore_signal(barrier, inc=1, device_id={"head": lax.rem(head + o, peers)}, device_id_type=MESH)
-    others = [after, before, mirror]
-    others += [base + lax.rem(place + o, GROUP) for o in range(1, GROUP)]
-    others += [lax.rem(x + o, rows_x) * ZROW + z for o in range(1, rows_x)]
+    others = [after, before]
     for s in others:
         pl.semaphore_signal(barrier, inc=1, device_id={"seq": s}, device_id_type=MESH)
 
@@ -198,6 +186,34 @@
     for o, copy in enumerate(copies):
         copy.wait_recv()
         g = g + parts[o]
+    g_out[...] = g
+    for copy in copies + halos:
+        copy.wait_send()
+
+
+def scan_kernel(heads, rows_x, scale, bias, g_in, uq, uk, uv, kk, qk, out,
+                attend, wu, xs, ms, rhi, rlo,
+                gathered, prefix, mine, other, total, tin, ein, begin, enext, full, staged, arrived,
+                send1, recv1, send2, recv2, send3, recv3, send4, recv4):
+    seq = lax.axis_index("seq")
+    z, x = lax.rem(seq, ZROW), seq // ZROW
+    half, place = z // GROUP, lax.rem(z, GROUP)
+    first_half = half == 0
+    base = seq - place
+    mirror = x * ZROW + (ZROW - 1 - z)
+    own = owned_at(jnp.where(first_half, place, GROUP - 1 - place))
+    seats = [jnp.where(first_half, SEAT[h], GROUP - 1 - SEAT[h]) for h in range(heads)]
+    key_heads, blocks = kk.shape[0], kk.shape[1]
+    group = heads // key_heads
+    shared = functools.partial(pltpu.make_async_remote_copy, device_id_type=MESH)
+
+    barrier = pltpu.get_barrier_semaphore()
+    others = [mirror]
+    others += [base + lax.rem(place + o, GROUP) for o in range(1, GROUP)]
+    others += [lax.rem(x + o, rows_x) * ZROW + z for o in range(1, rows_x)]
+    for s in others:
+        pl.semaphore_signal(barrier, inc=1, device_id={"seq": s}, device_id_type=MESH)
+    g = g_in[...]
 
     r, c = iota((C, C), 0), iota((C, C), 1)
     causal, strict = r >= c, r > c
@@ -293,6 +309,7 @@
                 out[at, cols] = rest
 
     maps(0)
+    pl.semaphore_wait(barrier, len(others))
     hand_over(0)
     maps(1)
     hand_over(1)
@@ -405,7 +422,7 @@
         cols = slice(h * DK, (h + 1) * DK)
         out[:, cols] = out[:, cols] + mm((rhi[:, cols], rlo[:, cols]), split(arrived[h]))
 
-    for copy in copies + halos + [to_mirror(0), to_mirror(1)] + last:
+    for copy in [to_mirror(0), to_mirror(1)] + last:
         copy.wait_send()
     for h in range(heads):
         @pl.when(place != seats[h])
@@ -444,29 +461,45 @@
         def f32(*shape):
             return pltpu.VMEM(shape, F32)
 
-        return pl.pallas_call(
-            functools.partial(whole_kernel, peers, heads, rows_x),
-            out_shape=jax.ShapeDtypeStruct((rows, heads * DV), F32),
-            in_specs=[smem] * 2 + [vm] * 3 + [pl.BlockSpec(memory_space=pltpu.HBM)] * 5,
-            out_specs=vm,
+        def result(*shape):
+            return jax.ShapeDtypeStruct(shape, F32)
+
+        def pinned(*arrays):
+            return [pltpu.with_memory_space_constraint(a, pltpu.HBM) for a in arrays]
+
+        made = pl.pallas_call(
+            functools.partial(features_kernel, peers, heads),
+            out_shape=(result(per, rows), result(*q.shape), result(*k.shape), result(*v.shape),
+                       result(key_heads, blocks, *square), result(key_heads, blocks, *square)),
+            in_specs=[vm] * 3 + [pl.BlockSpec(memory_space=pltpu.HBM)] * 5,
+            out_specs=(vm,) * 6,
             scratch_shapes=[
                 *(pltpu.VMEM(a.shape, BF16) for a in (hid, proj, q, k, v)), dma((5,)),
                 f32(peers, per, rows), f32(peers - 1, per, rows), pltpu.VMEM((HALO, width), BF16),
-                f32(rows + 8, width), f32(*q.shape), f32(*k.shape), f32(*v.shape),
-                f32(key_heads, blocks, *square), f32(key_heads, blocks, *square),
+                f32(rows + 8, width),
+                dma((peers - 1,)), dma((peers - 1,)), dma((3,)), dma((3,)),
+            ],
+            compiler_params=pltpu.CompilerParams(collective_id=0, has_side_effects=True, vmem_limit_bytes=24 * 1024 * 1024),
+            name="features",
+        )(*pinned(cq, ck, cv, hid, proj, q, k, v))
+        return pl.pallas_call(
+            functools.partial(scan_kernel, heads, rows_x),
+            out_shape=result(rows, heads * DV),
+            in_specs=[smem] * 2 + [vm] * 6,
+            out_specs=vm,
+            scratch_shapes=[
                 f32(heads, blocks, *square), f32(heads, blocks, C, DK + DV),
                 f32(heads, blocks - 1, DK, DK + DV), f32(heads, *pair),
                 pltpu.VMEM((rows, heads * DK), BF16), pltpu.VMEM((rows, heads * DK), BF16),
                 f32(GROUP, *pair), f32(GROUP - 1, *pair), f32(*pair), f32(*pair), f32(*pair), f32(*pair),
                 f32(DK, DV), f32(*pair), f32(DK, DV), f32(GROUP, DK, DK + DV),
                 f32(GROUP, DK, DV), f32(GROUP, DK, DV),
-                dma((peers - 1,)), dma((peers - 1,)), dma((3,)), dma((3,)),
                 dma((heads,)), dma((GROUP,)), dma((2,)), dma((2,)), dma((2,)), dma((2,)),
                 dma((GROUP - 1,)), dma((GROUP,)),
             ],
-            compiler_params=pltpu.CompilerParams(collective_id=0, has_side_effects=True, vmem_limit_bytes=40 * 1024 * 1024),
-            name="delta",
-        )(*(pltpu.with_memory_space_constraint(a, pltpu.HBM) for a in (scale, bias, cq, ck, cv, hid, proj, q, k, v)))
+            compiler_params=pltpu.CompilerParams(collective_id=1, has_side_effects=True, vmem_limit_bytes=36 * 1024 * 1024),
+            name="scan",
+        )(*pinned(scale, bias), *made)
 
     placed = (
         P("seq", "head"), P("head", None), P("seq", "head"), P("seq", "head"), P("seq", "head"),

time: 50.1 us -> 49.2 us (0.982)
  Pallas kernels: 48.9 us -> 48.1 us
    pallas_call x1 -> x2, Pallas kernels: 48.9 us -> 48.1 us  [the longest x1 35.2 us: per_device(): pl.pallas_call(functools.partial(scan_kernel, heads, rows_x), out_shape=r...]
where the time goes in v6:
time: 49.2 us; the launch traced here: 49.1 us
  Pallas kernels  48.1 us (98%)
  local copies, waits for them, and re-layouts  0.97 us (2%)
    pallas_call x1, Pallas kernels, per_device(): pl.pallas_call(functools.partial(scan_kernel, heads, rows_x), out_shape=r...  35.2 us
    pallas_call x1, Pallas kernels, per_device(): pl.pallas_call(functools.partial(features_kernel, peers, heads), out_shap...  12.9 us

profile of v6, /device:TPU:6, one launch (start us, length us, event | category | flops | bytes accessed | tf_op | source)
XLA Modules:
  0.0 49.1 jit_solution(17437162553418809238)
XLA Ops:
  0.0 12.9 %features.1 = (f32[8,512]{1,0:T(8,128)S(1)}, f32[512,256]{1,0:T(8,128)S(1)}, f32[512,256]{1,0:T(8,128)S(1)}, f32[512,512]{1,0:T(8,128)S(1)}, f32[2,4,128,128]{3,...) custom-call(bf16[4,256]{1,0:T(4,128)(2,1)} %cq.1, bf16[4,256]{1,0:T(4,128)(2,1)} %ck.1, bf16[4,512]{1,0:T(4,128)(2,1)} %cv.1, ...), custom_call_target="tpu_custom_call" | custom-call | tf_op jit(solution)/shard_map/features/pallas_call | solution.py:470
  12.9 35.2 %scan.1 = f32[512,512]{1,0:T(8,128)S(1)} custom-call(f32[4]{0:T(128)} %scale.1, f32[4]{0:T(128)} %bias.1, f32[8,512]{1,0:T(8,128)S(1)} %get-tuple-element.11.g_in, f32[512,256]{1,0:T(8,128)S(1)} %get-tuple-element.12.uq, f32[512,256]{1,0:T(8,128)S(1)} %get-tuple-element.13.uk, f32[512,512]{1,0:T(8,128)S(1)} %get-tuple-element.14.uv, ...), custom_call_target="tpu_custom_call" | custom-call | tf_op jit(solution)/shard_map/scan/pallas_call | solution.py:485
  48.1 1.0 %copy.12 = f32[512,512]{1,0:T(8,128)} copy(f32[512,512]{1,0:T(8,128)S(1)} %scan.1) | data formatting | bytes 2097152

commit v7 on v6

--- a/solution.py
+++ b/solution.py
@@ -192,8 +192,8 @@
 
 
 def scan_kernel(heads, rows_x, scale, bias, g_in, uq, uk, uv, kk, qk, out,
-                attend, wu, xs, ms, rhi, rlo,
-                gathered, prefix, mine, other, total, tin, ein, begin, enext, full, staged, arrived,
+                attend, wu, xs, third, ms, rhi, rlo,
+                gathered, prefix, mine, other, total, tin, ein, begin, enext, full, fhi, flo, staged, arrived,
                 send1, recv1, send2, recv2, send3, recv3, send4, recv4):
     seq = lax.axis_index("seq")
     z, x = lax.rem(seq, ZROW), seq // ZROW
@@ -266,13 +266,20 @@
             last = cum[b * width + h:b * width + h + 1, C - 1:C]
             pair = mm(split(keys_t[b] * jnp.exp(last - decay_row(h, b))), split(y))
             steps[h, b] = (jnp.exp(last) * eye - pair[:, :DK], pair[:, DK:])
-        for h in range(n * group, (n + 1) * group):
-            now = jnp.concatenate(steps[h, 0], axis=1)
-            for b in range(1, blocks):
-                xs[h, b - 1] = now
-                move, state = then(*steps[h, b], now)
-                now = jnp.concatenate([move, state], axis=1)
-            ms[h, 0], ms[h, 1] = now[:, :DK], now[:, DK:]
+        mine_now = range(n * group, (n + 1) * group)
+        for level in range(blocks // 2):
+            pair = {}
+            for h in mine_now:
+                b = 2 * level
+                now = jnp.concatenate(steps[h, b], axis=1)
+                pair[h] = then(*steps[h, b + 1], now)
+                if level == 0:
+                    xs[h, 0], xs[h, 1] = now, jnp.concatenate(pair[h], axis=1)
+                else:
+                    third[h] = now
+            tops = pair if level == 0 else {h: then(*pair[h], jnp.concatenate(tops[h], axis=1)) for h in mine_now}
+        for h in mine_now:
+            ms[h, 0], ms[h, 1] = tops[h]
 
     def to_owner(h):
         return shared(src_ref=ms.at[h], dst_ref=gathered.at[place], send_sem=send1.at[h],
@@ -299,7 +306,11 @@
                     got = mm(split(attend[h, b]), split(y))
                     response, rest = queries - got[:, :DK], got[:, DK:]
                 else:
-                    now = xs[h, b - 1]
+                    if b < blocks - 1:
+                        now = xs[h, b - 1]
+                    else:
+                        now = third[h]
+                        now = jnp.concatenate(then(now[:, :DK], now[:, DK:], xs[h, b - 2]), axis=1)
                     z = mm(split(y[:, :DK]), split(now))
                     y = jnp.concatenate([-z[:, :DK], y[:, DK:] - z[:, DK:]], axis=1)
                     got = mm(split(jnp.concatenate([queries, attend[h, b]], axis=1)),
@@ -381,10 +392,13 @@
         begin[0], begin[1] = then(begin[0], begin[1], wide(tin))
 
     start_s = split(wide(begin))
-    full[0] = wide(begin)
+    fhi[0:DK, :], flo[0:DK, :] = start_s[0][:, :DK], start_s[1][:, :DK]
+    full[0:DK, :] = begin[1]
     for t in range(1, GROUP):
         y = mm(split(prefix[t - 1, 0]), start_s)
-        full[t] = jnp.concatenate([y[:, :DK], y[:, DK:] + prefix[t - 1, 1]], axis=1)
+        at = slice(t * DK, (t + 1) * DK)
+        fhi[at, :], flo[at, :] = split(y[:, :DK])
+        full[at, :] = y[:, DK:] + prefix[t - 1, 1]
 
     @pl.when(x == 0)
     def _():
@@ -402,17 +416,15 @@
 
     e_s = split(ein[...])
 
-    def stage(t):
-        staged[t] = mm(split(full[t, :, :DK]), e_s) + full[t, :, DK:]
-
+    y = mm((fhi[...], flo[...]), e_s) + full[...]
+    for t in range(GROUP):
+        staged[t] = y[t * DK:(t + 1) * DK]
     last = []
     for o in range(1, GROUP):
         p = lax.rem(place + o, GROUP)
-        stage(p)
         last.append(shared(src_ref=staged.at[p], dst_ref=arrived.at[own], send_sem=send4.at[o - 1],
                            recv_sem=recv4.at[own], device_id={"seq": base + p}))
         last[-1].start()
-    stage(place)
     arrived[own] = staged[place]
     for h in range(heads):
         @pl.when(own != h)
@@ -451,7 +463,7 @@
     def per_device(hid, proj, q, k, v, cq, ck, cv, scale, bias):
         heads, rows = scale.shape[0], q.shape[0]
         key_heads, blocks = q.shape[1] // DK, rows // C
-        assert heads == GROUP and rows == blocks * C
+        assert heads == GROUP and blocks == 4 and rows == blocks * C
         width = q.shape[1] + k.shape[1] + v.shape[1]
         per = proj.shape[1] // peers
         proj = jnp.transpose(proj)
@@ -489,10 +501,11 @@
             out_specs=vm,
             scratch_shapes=[
                 f32(heads, blocks, *square), f32(heads, blocks, C, DK + DV),
-                f32(heads, blocks - 1, DK, DK + DV), f32(heads, *pair),
+                f32(heads, blocks - 2, DK, DK + DV), f32(heads, DK, DK + DV), f32(heads, *pair),
                 pltpu.VMEM((rows, heads * DK), BF16), pltpu.VMEM((rows, heads * DK), BF16),
                 f32(GROUP, *pair), f32(GROUP - 1, *pair), f32(*pair), f32(*pair), f32(*pair), f32(*pair),
-                f32(DK, DV), f32(*pair), f32(DK, DV), f32(GROUP, DK, DK + DV),
+                f32(DK, DV), f32(*pair), f32(DK, DV), f32(GROUP * DK, DV),
+                pltpu.VMEM((GROUP * DK, DK), BF16), pltpu.VMEM((GROUP * DK, DK), BF16),
                 f32(GROUP, DK, DV), f32(GROUP, DK, DV),
                 dma((heads,)), dma((GROUP,)), dma((2,)), dma((2,)), dma((2,)), dma((2,)),
                 dma((GROUP - 1,)), dma((GROUP,)),

time: 49.2 us -> 48.6 us (0.988)
  Pallas kernels: 48.1 us -> 47.4 us
    pallas_call x1, Pallas kernels: 35.2 us -> 34.5 us  [per_device(): pl.pallas_call(functools.partial(scan_kernel, heads, rows_x), out_shape=r...]
where the time goes in v7:
time: 48.6 us; the launch traced here: 48.4 us
  Pallas kernels  47.4 us (98%)
  local copies, waits for them, and re-layouts  0.97 us (2%)
    pallas_call x1, Pallas kernels, per_device(): pl.pallas_call(functools.partial(scan_kernel, heads, rows_x), out_shape=r...  34.5 us
    pallas_call x1, Pallas kernels, per_device(): pl.pallas_call(functools.partial(features_kernel, peers, heads), out_shap...  12.9 us
    unnamed x1, local copies, waits for them, and re-layouts  0.97 us

profile of v7, /device:TPU:6, one launch (start us, length us, event | category | flops | bytes accessed | tf_op | source)
XLA Modules:
  0.0 48.4 jit_solution(7084096471324649223)
XLA Ops:
  0.0 12.9 %features.1 = (f32[8,512]{1,0:T(8,128)S(1)}, f32[512,256]{1,0:T(8,128)S(1)}, f32[512,256]{1,0:T(8,128)S(1)}, f32[512,512]{1,0:T(8,128)S(1)}, f32[2,4,128,128]{3,...) custom-call(bf16[4,256]{1,0:T(4,128)(2,1)} %cq.1, bf16[4,256]{1,0:T(4,128)(2,1)} %ck.1, bf16[4,512]{1,0:T(4,128)(2,1)} %cv.1, ...), custom_call_target="tpu_custom_call" | custom-call | tf_op jit(solution)/shard_map/features/pallas_call | solution.py:482
  12.9 34.5 %scan.1 = f32[512,512]{1,0:T(8,128)S(1)} custom-call(f32[4]{0:T(128)} %scale.1, f32[4]{0:T(128)} %bias.1, f32[8,512]{1,0:T(8,128)S(1)} %get-tuple-element.11.g_in, f32[512,256]{1,0:T(8,128)S(1)} %get-tuple-element.12.uq, f32[512,256]{1,0:T(8,128)S(1)} %get-tuple-element.13.uk, f32[512,512]{1,0:T(8,128)S(1)} %get-tuple-element.14.uv, ...), custom_call_target="tpu_custom_call" | custom-call | tf_op jit(solution)/shard_map/scan/pallas_call | solution.py:497
  47.4 1.0 %copy.12 = f32[512,512]{1,0:T(8,128)} copy(f32[512,512]{1,0:T(8,128)S(1)} %scan.1) | data formatting | bytes 2097152

commit v8 on v7

--- a/solution.py
+++ b/solution.py
@@ -146,7 +146,7 @@
         halos.append(shared(src_ref=src.at[pl.ds(rows - HALO, HALO)],
                             dst_ref=halo.at[:, pl.ds(col, src.shape[1])],
                             send_sem=hsend.at[i], recv_sem=hrecv.at[i], device_id={"seq": after}))
-    for copy in halos + copies:
+    for copy in [copies[i] for i in (3, 2, 4, 1, 5, 0, 6)] + halos:
         copy.start()
 
     for src, col in columns:
@@ -350,7 +350,6 @@
     prefix[0, 0], prefix[0, 1] = gathered[0, 0], gathered[0, 1]
     prefix[1, 0], prefix[1, 1] = early[:, :DK], early[:, DK:]
     prefix[2, 0], prefix[2, 1] = then(gathered[2, 0], gathered[2, 1], early)
-    responses(1)
 
     @pl.when(first_half)
     def _():
@@ -399,6 +398,8 @@
         at = slice(t * DK, (t + 1) * DK)
         fhi[at, :], flo[at, :] = split(y[:, :DK])
         full[at, :] = y[:, DK:] + prefix[t - 1, 1]
+
+    responses(1)
 
     @pl.when(x == 0)
     def _():

time: 48.6 us -> 48.1 us (0.990)
  Pallas kernels: 47.4 us -> 46.9 us
    pallas_call x1, Pallas kernels: 34.5 us -> 34 us  [per_device(): pl.pallas_call(functools.partial(scan_kernel, heads, rows_x), out_shape=r...]
where the time goes in v8:
time: 48.1 us; the launch traced here: 47.9 us
  Pallas kernels  46.9 us (98%)
  local copies, waits for them, and re-layouts  0.97 us (2%)
    pallas_call x1, Pallas kernels, per_device(): pl.pallas_call(functools.partial(scan_kernel, heads, rows_x), out_shape=r...  34 us
    pallas_call x1, Pallas kernels, per_device(): pl.pallas_call(functools.partial(features_kernel, peers, heads), out_shap...  12.9 us
    unnamed x1, local copies, waits for them, and re-layouts  0.97 us

profile of v8, /device:TPU:6, one launch (start us, length us, event | category | flops | bytes accessed | tf_op | source)
XLA Modules:
  0.0 47.9 jit_solution(1844748630712744128)
XLA Ops:
  0.0 12.9 %features.1 = (f32[8,512]{1,0:T(8,128)S(1)}, f32[512,256]{1,0:T(8,128)S(1)}, f32[512,256]{1,0:T(8,128)S(1)}, f32[512,512]{1,0:T(8,128)S(1)}, f32[2,4,128,128]{3,...) custom-call(bf16[4,256]{1,0:T(4,128)(2,1)} %cq.1, bf16[4,256]{1,0:T(4,128)(2,1)} %ck.1, bf16[4,512]{1,0:T(4,128)(2,1)} %cv.1, ...), custom_call_target="tpu_custom_call" | custom-call | tf_op jit(solution)/shard_map/features/pallas_call | solution.py:483
  12.9 34.0 %scan.1 = f32[512,512]{1,0:T(8,128)S(1)} custom-call(f32[4]{0:T(128)} %scale.1, f32[4]{0:T(128)} %bias.1, f32[8,512]{1,0:T(8,128)S(1)} %get-tuple-element.11.g_in, f32[512,256]{1,0:T(8,128)S(1)} %get-tuple-element.12.uq, f32[512,256]{1,0:T(8,128)S(1)} %get-tuple-element.13.uk, f32[512,512]{1,0:T(8,128)S(1)} %get-tuple-element.14.uv, ...), custom_call_target="tpu_custom_call" | custom-call | tf_op jit(solution)/shard_map/scan/pallas_call | solution.py:498
  46.9 1.0 %copy.12 = f32[512,512]{1,0:T(8,128)} copy(f32[512,512]{1,0:T(8,128)S(1)} %scan.1) | data formatting | bytes 2097152
